TPU v7x, 256 devices: a whole 4x4x8 slice. The times are simulated.
256 devices in a mesh: vx: 16 (over y, x), vy: 8 (over z), subj: 2 (over core).
Axes of the slice: x: 4, y: 4, z: 8, core: 2. Of those that a mesh axis runs over, the one named last changes fastest.
Arguments:
- volumes: bfloat16 [8, 64, 32, 64, 128], P('subj', None, 'vx', 'vy'), may hold values from -24 to 24
- flip_bits: int32 [32, 64, 128], P('vx', 'vy'), may hold values from 0 to 1
- hadamard_block: int32 [4096], replicated, may hold values from 0 to 127
- stratum_offset: int32 [4096], replicated, may hold values from 0 to 15
- subject_order: int32 [8], replicated, may hold values from 0 to 7, each once
Outputs:
- sketch: float32 [4096, 512], P(('vx', 'vy'), 'subj')
- gram: float32 [512, 512], P('subj')
Inputs may be any that keep to these rules, and one draw needn't show every extreme that they name: `subject_order`: each of 0 to 7 appears once.
All inputs are finite; a program needn't handle non-finite values.
Results may differ from a plain program's by a relative error of at most 0.0003.
Values may be sent and summed in bfloat16 or wider, within the bound.
A program may use at most 64 MiB of HBM per device.

v0:
```python
import math

import jax
import jax.numpy as jnp
from jax import lax
from jax.sharding import PartitionSpec as P

KD = 32


w_side = 0.2741
w_mid = 0.4518


def padded_2(cells, sides, width):
    for axis, dim in sides:
        count = lax.axis_size(axis)
        ends = count - 1
        head = lax.slice_in_dim(cells, 0, width, axis=dim)
        tail = lax.slice_in_dim(cells, cells.shape[dim] - width, cells.shape[dim], axis=dim)
        cells = jnp.concatenate(
            [
                lax.ppermute(tail, axis, [(i, (i + 1) % count) for i in range(ends)]),
                cells,
                lax.ppermute(head, axis, [((i + 1) % count, i) for i in range(ends)]),
            ],
            axis=dim,
        )
    return cells


def hadamard_sign(first, second, nbits):
    parity = jnp.zeros_like(first + second, dtype=jnp.int32)
    for level in range(nbits):
        parity = parity + first // (1 << level) % 2 * (second // (1 << level) % 2)
    return (1 - 2 * (parity % 2)).astype(jnp.float32)


def hadamard_table(order):
    index = jnp.arange(order, dtype=jnp.int32)
    return hadamard_sign(index[:, None], index[None, :], order.bit_length() - 1)


def smooth_axis(padded, axis):
    length = padded.shape[axis]
    lower = lax.slice_in_dim(padded, 0, length - 2, axis=axis)
    centre = lax.slice_in_dim(padded, 1, length - 1, axis=axis)
    upper = lax.slice_in_dim(padded, 2, length, axis=axis)
    return w_side * (lower + upper) + w_mid * centre


def on_device(volumes, flip_bits, hadamard_block, stratum_offset, subject_order):
    highest_level = lax.Precision.HIGHEST
    groups = lax.axis_size(("vx", "vy"))
    group_bits = groups.bit_length() - 1
    group_index = lax.axis_index(("vx", "vy"))
    subj_dev, trs, cx_dev, cy_dev, depth = volumes.shape
    local_rows = cx_dev * cy_dev * depth
    stratum = local_rows // groups
    block_width = subj_dev * trs
    scale = 1.0 / math.sqrt(local_rows * groups)
    padded = padded_2(volumes, (("vx", 2), ("vy", 3)), 1).astype(jnp.float32)
    across = smooth_axis(padded, 2)
    along = smooth_axis(across, 3)
    deeper = jnp.pad(along, ((0, 0), (0, 0), (0, 0), (0, 0), (1, 1)))
    smoothed = smooth_axis(deeper, 4)
    signs = (2 * flip_bits - 1).astype(jnp.float32)
    flipped_signs = (smoothed * signs[None, None]).reshape(block_width, cx_dev * cy_dev, depth)
    first_table = hadamard_table(cx_dev * cy_dev)
    second_table = hadamard_table(depth)
    half_span = jnp.einsum("hd,ndw->nhw", first_table, flipped_signs, precision=highest_level)
    mixed_rows = jnp.einsum(
        "vza,sa->vzs", half_span, second_table, precision=highest_level
    ).reshape(block_width, local_rows)
    own_offsets = lax.dynamic_slice_in_dim(stratum_offset, group_index * KD, KD)
    own_blocks = lax.dynamic_slice_in_dim(hadamard_block, group_index * KD, KD)
    selector = (own_offsets[:, None] == jnp.arange(stratum, dtype=jnp.int32)[None, :]).astype(
        jnp.float32
    )
    block_signs = hadamard_sign(
        own_blocks[:, None], jnp.arange(groups, dtype=jnp.int32)[None, :], group_bits
    )
    picked = jnp.einsum(
        "cdm,rm->crd",
        lax.all_to_all(
            mixed_rows.reshape(block_width, groups, stratum),
            ("vx", "vy"),
            split_axis=1,
            concat_axis=1,
            tiled=True,
        ),
        selector,
        precision=highest_level,
    )
    summed = jnp.einsum("crd,rd->rc", picked, block_signs, precision=highest_level)
    sketch_block = summed * scale
    whole = lax.all_gather(sketch_block, "subj", axis=1, tiled=True)
    total_cols = whole.shape[1]
    subjects = total_cols // trs
    columns = jnp.arange(total_cols, dtype=jnp.int32)
    subject_of = columns // trs
    position = jnp.sum(
        jnp.where(
            subject_of[:, None] == jnp.arange(subjects, dtype=jnp.int32)[None, :],
            subject_order[None, :],
            0,
        ),
        axis=1,
    )
    target = position * trs + columns % trs
    mover = (target[:, None] == columns[None, :]).astype(jnp.float32)
    ordered = jnp.dot(whole, mover, precision=highest_level)
    mine = lax.dynamic_slice_in_dim(ordered, lax.axis_index("subj") * block_width, block_width, 1)
    partial_gram = jnp.dot(mine.T, ordered, precision=highest_level)
    gram_block = lax.psum(partial_gram, ("vx", "vy")) / (KD * groups)
    return (sketch_block, gram_block)


def solution(mesh):
    placed = (P("subj", None, "vx", "vy", None), P("vx", "vy", None), P(), P(), P())
    return jax.shard_map(
        on_device,
        mesh=mesh,
        in_specs=placed,
        out_specs=(P(("vx", "vy"), "subj"), P("subj", None)),
        check_vma=False,
    )
```

profile of v0, /device:TPU:1, one launch (start us, length us, event | category | flops | bytes accessed | tf_op | source)
XLA Modules:
  0.0 352.5 jit_solution(1760441476699427427)
XLA Ops:
  7.2 0.0 copy-start
  7.2 1.4 fusion.102
  8.5 4.0 %collective-permute-start = (bf16[4,64,1,8,128]{4,3,2,1,0:T(8,128)(2,1)S(1)}, bf16[4,64,1,8,128]{4,3,2,1,0:T(8,128)(2,1)S(1)}, u32[]{:S(2)}, u32[]{:S(2)}) collective-permute-start(bf16[4,64,1,8,128]{4,3,2,1,0:T(8,128)(2,1)S(1)} %get-tuple-element.10), channel_id=1, source_target_pairs={{0,16},{16,32},{32,48},{48,64},{64,80},{80,96},{96,112},{112,128},... | collective-permute-start | bytes 1572872 | tf_op jit(solution)/shard_map/ppermute | solution.py:23
  12.5 1.3 collective-permute-start.1
  13.9 9.2 %collective-permute-done = bf16[4,64,1,8,128]{4,3,2,1,0:T(8,128)(2,1)S(1)} collective-permute-done((bf16[4,64,1,8,128]{4,3,2,1,0:T(8,128)(2,1)S(1)}, bf16[4,64,1,8,128]{4,3,2,1,0:T(8,128)(2,1)S(1)}, u32[]{:S(2)}, u32[]{:S(2)}) %collective-permute-start) | collective-permute-done | bytes 524320 | tf_op jit(solution)/shard_map/ppermute | solution.py:23
  23.1 0.1 constant_dynamic-update-slice_fusion.2
  23.2 0.0 copy-done
  23.2 0.3 constant_dynamic-update-slice_fusion.1
  23.4 3.5 collective-permute-done.1
  26.9 0.1 constant_dynamic-update-slice_fusion
  27.1 0.0 copy-start.2
  27.1 0.7 fusion.101
  27.8 0.1 copy.29
  27.8 3.6 %collective-permute-start.2 = (bf16[4,64,4,1,128]{4,1,3,2,0:T(8,128)(2,1)S(1)}, bf16[4,64,4,1,128]{4,1,3,2,0:T(8,128)(2,1)S(1)}, u32[]{:S(2)}, u32[]{:S(2)}) collective-permute-start(bf16[4,64,4,1,128]{4,1,3,2,0:T(8,128)(2,1)S(1)} %copy.29), channel_id=1, source_target_pairs={{0,2},{2,4},{4,6},{6,8},{8,10},{10,12},{12,14},{1,3},{3,5},{5,7},{... | collective-permute-start | bytes 786440 | tf_op jit(solution)/shard_map/ppermute | solution.py:23
  31.4 0.1 copy.30
  31.5 1.3 collective-permute-start.3
  32.8 0.0 copy-done.2
  32.8 2.4 collective-permute-done.2
  35.2 0.4 copy.31
  35.6 3.8 %collective-permute-done.3 = bf16[4,64,4,1,128]{4,1,3,2,0:T(8,128)(2,1)S(1)} collective-permute-done((bf16[4,64,4,1,128]{4,1,3,2,0:T(8,128)(2,1)S(1)}, bf16[4,64,4,1,128]{4,1,3,2,0:T(8,128)(2,1)S(1)}, u32[]{:S(2)}, u32[]{:S(2)}) %collective-permute-start.3) | collective-permute-done | bytes 262176 | tf_op jit(solution)/shard_map/ppermute | solution.py:25
  39.5 0.4 copy.32
  39.9 2.4 maximum_convert_fusion
  42.3 1.1 fusion
  43.3 0.5 fusion.8
  43.9 1.1 fusion.7
  45.0 1.9 convolution_bitcast_fusion.1
  47.0 3.9 %fusion.10 = f32[256,16,128]{0,2,1:T(8,128)} fusion(f32[256,16,128]{2,1,0:T(8,128)S(1)} %convolution_bitcast_fusion.1, s32[128]{0:T(128)S(1)} %get-tuple-element.16, s32[128]{0:T(128)S(1)} %get-tuple-element.17, s32[128]{0:T(128)S(1)} %get-tuple-element.18, s32[128]{0:T(128)S(1)} %get-tuple-element.19, s32[128]{0:T(128)S(1)} %get-tuple-element.20, ...), kind=kOutput, calls=%fused_computation.18 | convolution fusion | flops 805748736 | bytes 4197888 | tf_op jit(solution)/shard_map/vza,sa->vzs/dot_general | solution.py:72
  50.9 0.0 copy-start.3
  50.9 17.4 %all-to-all-start = ((f32[256,128,16]{0,2,1:T(8,128)}), f32[256,128,16]{0,2,1:T(8,128)}, u32[]{:S(2)}, u32[]{:S(2)}) async-start(f32[256,128,16]{0,2,1:T(8,128)} %bitcast.5), calls=%async_computation | async-start | bytes 4194304 | tf_op jit(solution)/shard_map/all_to_all | solution.py:85
  68.3 0.0 all-reduce.3.cloned.1.call-start
  68.4 0.8 dynamic_slice.9
  69.1 0.8 and_select_fusion.12
  69.9 0.0 copy-done.3
  69.9 0.1 select_reduce_fusion
  70.0 0.8 and_select_fusion.10
  70.8 0.1 fusion.45
  70.9 47.3 %all-to-all-done = f32[256,128,16]{0,2,1:T(8,128)} async-done(((f32[256,128,16]{0,2,1:T(8,128)}), f32[256,128,16]{0,2,1:T(8,128)}, u32[]{:S(2)}, u32[]{:S(2)}) %all-to-all-start) | async-done | bytes 2097184 | tf_op jit(solution)/shard_map/all_to_all | solution.py:85
  118.3 2.5 copy.34
  120.8 1.9 convolution_bitcast_fusion
  122.7 6.0 %fusion.2 = f32[32,1,256]{2,1,0:T(1,128)S(1)} fusion(f32[32,128,1]{1,2,0:T(1,128)S(1)} %bitcast.26, f32[256,32,128]{2,1,0:T(8,128)S(1)} %convolution_bitcast_fusion), kind=kOutput, calls=%fused_computation.7 | convolution fusion | flops 12582912 | bytes 4243456 | tf_op jit(solution)/shard_map/crd,rd->rc/dot_general | solution.py:95
  128.7 0.0 copy-start.1
  128.7 6.5 %all_gather.3 = f32[32,512]{1,0:T(8,128)S(1)} all-gather(f32[32,256]{1,0:T(8,128)S(1)} %bitcast_multiply_fusion), channel_id=1, replica_groups=mesh['vx'=16,'vy'=8,'subj'=2] {'subj'}, dimensions={1}, use_global_device_ids=true | all-gather | bytes 98304 | tf_op jit(solution)/shard_map/all_gather | solution.py:97
  135.2 0.5 fusion.12
  135.7 1.4 fusion.23
  137.1 0.0 all-reduce.3.cloned.1.call-update
  137.2 206.6 %all-reduce.3.cloned.1.call-done = f32[256,512]{1,0:T(8,128)} async-done(((f32[256,512]{1,0:T(8,128)}), f32[256,512]{1,0:T(8,128)}) %all-reduce.3.cloned.1.call-update) | async-done | bytes 524304 | tf_op jit(solution)/shard_map/psum | solution.py:115
  343.7 1.9 broadcast_multiply_fusion
  345.6 0.0 copy-done.1
  (11 shorter events, 0.1 us)
Async XLA Ops:
  7.2 16.0 %copy-start = (bf16[4,64,2,8,128]{4,3,2,1,0:T(8,128)(2,1)S(1)}, bf16[4,64,2,8,128]{4,3,2,1,0:T(8,128)(2,1)}, u32[]{:S(2)}) copy-start(bf16[4,64,2,8,128]{4,3,2,1,0:T(8,128)(2,1)} %param.5) | copy-start | bytes 3145732
  8.5 14.5 %collective-permute-start = (bf16[4,64,1,8,128]{4,3,2,1,0:T(8,128)(2,1)S(1)}, bf16[4,64,1,8,128]{4,3,2,1,0:T(8,128)(2,1)S(1)}, u32[]{:S(2)}, u32[]{:S(2)}) collective-permute-start(bf16[4,64,1,8,128]{4,3,2,1,0:T(8,128)(2,1)S(1)} %get-tuple-element.10), channel_id=1, source_target_pairs={{0,16},{16,32},{32,48},{48,64},{64,80},{80,96},{96,112},{112,128},... | collective-permute-start | bytes 1572872 | tf_op jit(solution)/shard_map/ppermute | solution.py:23
  12.5 14.4 %collective-permute-start.1 = (bf16[4,64,1,8,128]{4,3,2,1,0:T(8,128)(2,1)S(1)}, bf16[4,64,1,8,128]{4,3,2,1,0:T(8,128)(2,1)S(1)}, u32[]{:S(2)}, u32[]{:S(2)}) collective-permute-start(bf16[4,64,1,8,128]{4,3,2,1,0:T(8,128)(2,1)S(1)} %get-tuple-element.9), channel_id=1, source_target_pairs={{16,0},{32,16},{48,32},{64,48},{80,64},{96,80},{112,96},{128,112},... | collective-permute-start | bytes 1572872 | tf_op jit(solution)/shard_map/ppermute | solution.py:25
  27.1 5.7 %copy-start.2 = (s32[2,8,128]{2,1,0:T(8,128)S(1)}, s32[2,8,128]{2,1,0:T(8,128)}, u32[]{:S(2)}) copy-start(s32[2,8,128]{2,1,0:T(8,128)} %param.6) | copy-start | bytes 24580
  27.8 7.4 %collective-permute-start.2 = (bf16[4,64,4,1,128]{4,1,3,2,0:T(8,128)(2,1)S(1)}, bf16[4,64,4,1,128]{4,1,3,2,0:T(8,128)(2,1)S(1)}, u32[]{:S(2)}, u32[]{:S(2)}) collective-permute-start(bf16[4,64,4,1,128]{4,1,3,2,0:T(8,128)(2,1)S(1)} %copy.29), channel_id=1, source_target_pairs={{0,2},{2,4},{4,6},{6,8},{8,10},{10,12},{12,14},{1,3},{3,5},{5,7},{... | collective-permute-start | bytes 786440 | tf_op jit(solution)/shard_map/ppermute | solution.py:23
  31.5 8.0 %collective-permute-start.3 = (bf16[4,64,4,1,128]{4,1,3,2,0:T(8,128)(2,1)S(1)}, bf16[4,64,4,1,128]{4,1,3,2,0:T(8,128)(2,1)S(1)}, u32[]{:S(2)}, u32[]{:S(2)}) collective-permute-start(bf16[4,64,4,1,128]{4,1,3,2,0:T(8,128)(2,1)S(1)} %copy.30), channel_id=1, source_target_pairs={{2,0},{4,2},{6,4},{8,6},{10,8},{12,10},{14,12},{3,1},{5,3},{7,5},{... | collective-permute-start | bytes 786440 | tf_op jit(solution)/shard_map/ppermute | solution.py:25
  50.9 19.0 %copy-start.3 = (s32[8]{0:T(128)S(1)}, s32[8]{0:T(128)}, u32[]{:S(2)}) copy-start(s32[8]{0:T(128)} %param.9) | copy-start | bytes 100
  50.9 67.3 %all-to-all-start = ((f32[256,128,16]{0,2,1:T(8,128)}), f32[256,128,16]{0,2,1:T(8,128)}, u32[]{:S(2)}, u32[]{:S(2)}) async-start(f32[256,128,16]{0,2,1:T(8,128)} %bitcast.5), calls=%async_computation | async-start | bytes 4194304 | tf_op jit(solution)/shard_map/all_to_all | solution.py:85
  68.3 275.4 %all-reduce.3.cloned.1.call-start = ((), (), s32[]{:S(2)}) async-start(), calls=%async_computation.1 | async-start | bytes 1048576 | tf_op jit(solution)/shard_map/psum | solution.py:115
  128.7 216.9 %copy-start.1 = (f32[32,256]{1,0:T(8,128)}, f32[32,256]{1,0:T(8,128)S(1)}, u32[]{:S(2)}) copy-start(f32[32,256]{1,0:T(8,128)S(1)} %bitcast_multiply_fusion) | copy-start | bytes 98308
Sparse Core Ops, SparseCore 0:
  137.3 206.4 all-reduce.2
where the time goes:
time: 357 us; the launch traced here: 352 us
  waiting for transfers between devices  273 us (76%)
  starting transfers between devices  27.5 us (8%)
  matrix products  15.7 us (4%)
  between operations  14.3 us (4%)
  other arithmetic  8.81 us (2%)
  local copies, waits for them, and re-layouts  6.74 us (2%)
  blocking collectives  6.47 us (2%)
    psum x1, waiting for transfers between devices, on_device(): gram_block = lax.psum(partial_gram, ('vx', 'vy')) / (KD * groups)  207 us
    all_to_all x1, waiting for transfers between devices, on_device(): lax.all_to_all(mixed_rows.reshape(block_width, groups, stratum), ('vx', '...  47.3 us
    all_to_all x1, starting transfers between devices, on_device(): lax.all_to_all(mixed_rows.reshape(block_width, groups, stratum), ('vx', '...  17.4 us
    ppermute x2, waiting for transfers between devices, padded_2(): lax.ppermute(tail, axis, [(i, (i + 1) % count) for i in range(ends)])  11.6 us
    ppermute x2, starting transfers between devices, padded_2(): lax.ppermute(tail, axis, [(i, (i + 1) % count) for i in range(ends)])  7.52 us
    ppermute x2, waiting for transfers between devices, padded_2(): lax.ppermute(head, axis, [((i + 1) % count, i) for i in range(ends)])  7.34 us
  transfers between devices with their start and end apart: 6, of which 6 were waited for; matrix products, arithmetic and copies ran while one was open for 1% of the time, Pallas kernels for 0%

commit v1 on v0

v1 whole, which is shorter than its diff:
```python
import functools
import math

import jax
import jax.numpy as jnp
from jax import lax
from jax.experimental import pallas as pl
from jax.experimental.pallas import tpu as pltpu
from jax.sharding import PartitionSpec as P

MESH = pl.DeviceIdType.MESH
F32, BF16, I32 = jnp.float32, jnp.bfloat16, jnp.int32

w_side = 0.2741
w_mid = 0.4518

RX, RY, RZ = 4, 4, 8
PLANE = RX * RY
KD = 32
COLS = 256
HALF = 128
EX, EY = 4, 10
PLANES = EX * EY
STRATUM = 16


def split2(v):
    hi = v.astype(BF16)
    return hi, (v - hi.astype(F32)).astype(BF16)


def halo_kernel(flip_ref, ext_ref, buf, send_sem, recv_sem):
    vx, vy, sj = lax.axis_index("vx"), lax.axis_index("vy"), lax.axis_index("subj")
    offs = [(dx, dy) for dx in (-1, 0, 1) for dy in (-1, 0, 1) if (dx, dy) != (0, 0)]

    def dev(dx, dy):
        return (lax.rem(vx + dx + 16, 16), lax.rem(vy + dy + 8, 8), sj)

    barrier = pltpu.get_barrier_semaphore()
    for dx, dy in offs:
        pl.semaphore_signal(barrier, inc=1, device_id=dev(dx, dy), device_id_type=MESH)
    pl.semaphore_wait(barrier, len(offs))
    copies = []
    for i, (dx, dy) in enumerate(offs):
        copies.append(
            pltpu.make_async_remote_copy(
                src_ref=flip_ref,
                dst_ref=buf.at[i],
                send_sem=send_sem.at[i],
                recv_sem=recv_sem.at[i],
                device_id=dev(dx, dy),
                device_id_type=MESH,
            )
        )
    for c in copies:
        c.start()
    lo_x = jnp.where(vx > 0, 1, 0)
    hi_x = jnp.where(vx < 15, 1, 0)
    lo_y = jnp.where(vy > 0, 1, 0)
    hi_y = jnp.where(vy < 7, 1, 0)
    okx = {-1: lo_x, 0: 1, 1: hi_x}
    oky = {-1: lo_y, 0: 1, 1: hi_y}
    for x in range(2):
        for y in range(8):
            ext_ref[x + 1, y + 1] = (2 * flip_ref[x, pl.ds(y, 1), :] - 1).astype(F32)
    for c in copies:
        c.wait()
    for i, (dx, dy) in enumerate(offs):
        sx, sy = -dx, -dy
        ok = (okx[sx] * oky[sy]).astype(F32)
        xs = {-1: [(0, 1)], 0: [(1, 0), (2, 1)], 1: [(3, 0)]}[sx]
        ys = {-1: [(0, 7)], 0: [(k + 1, k) for k in range(8)], 1: [(9, 0)]}[sy]
        for ex, bx in xs:
            for ey, by in ys:
                ext_ref[ex, ey] = (2 * buf[i, bx, pl.ds(by, 1), :] - 1).astype(F32) * ok


def sign_halo(flip_bits):
    return pl.pallas_call(
        halo_kernel,
        out_shape=jax.ShapeDtypeStruct((EX, EY, 1, 128), F32),
        in_specs=[pl.BlockSpec(memory_space=pltpu.VMEM)],
        out_specs=pl.BlockSpec(memory_space=pltpu.VMEM),
        scratch_shapes=[
            pltpu.VMEM((8, 2, 8, 128), I32),
            pltpu.SemaphoreType.DMA((8,)),
            pltpu.SemaphoreType.DMA((8,)),
        ],
        compiler_params=pltpu.CompilerParams(collective_id=0, has_side_effects=True),
        name="sign_halo",
    )(flip_bits)


def local_kernel(vol_ref, ext_ref, rc_ref, so_ref, c_ref, zs, xs, tt_hi, tt_lo):
    vx, vy = lax.axis_index("vx"), lax.axis_index("vy")
    row = lax.broadcasted_iota(I32, (128, 128), 0)
    col = lax.broadcasted_iota(I32, (128, 128), 1)
    dist = jnp.abs(row - col)
    band = jnp.where(dist == 0, w_mid, jnp.where(dist == 1, w_side, 0.0)).astype(F32)
    wcat = jnp.concatenate(split2(band), axis=1)

    def smooth_z(i, _):
        v = vol_ref[pl.ds(i * 32, 32)].astype(F32).reshape(256, 128).astype(BF16)
        r = jnp.dot(v, wcat, preferred_element_type=F32)
        zs[pl.ds(i * 256, 256), :] = r[:, :128] + r[:, 128:]
        return 0

    lax.fori_loop(0, 16, smooth_z, 0)

    zero = jnp.zeros((COLS, 128), F32)
    for ex in range(EX):
        for y in (0, 1, 10, 11):
            xs[ex, y] = zero

    for y in range(8):
        a = zs[pl.ds(y, COLS, stride=16), :]
        b = zs[pl.ds(8 + y, COLS, stride=16), :]
        xs[0, y + 2] = w_side * a
        xs[1, y + 2] = w_mid * a + w_side * b
        xs[2, y + 2] = w_side * a + w_mid * b
        xs[3, y + 2] = w_side * b

    bits = row & col
    for s in (4, 2, 1):
        bits = bits ^ (bits >> s)
    hz = (1 - 2 * (bits & 1)).astype(F32).astype(BF16)
    hcat = jnp.concatenate([hz, hz], axis=1)

    def planes(yi, _):
        for ex in range(EX):
            f = w_side * (xs[ex, yi] + xs[ex, yi + 2]) + w_mid * xs[ex, yi + 1]
            f = f * ext_ref[ex, yi]
            fcat = jnp.concatenate(split2(f), axis=1)
            t = lax.dot_general(hcat, fcat, (((1,), (1,)), ((), ())), preferred_element_type=F32)
            thi, tlo = split2(t)
            at = pl.ds(pl.multiple_of((ex * EY + yi) * STRATUM, STRATUM), STRATUM)
            for g in range(RZ):
                tt_hi[g, at, :] = thi[g * STRATUM : (g + 1) * STRATUM, :]
                tt_lo[g, at, :] = tlo[g * STRATUM : (g + 1) * STRATUM, :]
        return 0

    lax.fori_loop(0, EY, planes, 0)

    lane = lax.broadcasted_iota(I32, (1, 128), 1)
    gx = vx * 2 + lane // EY - 1 + 32
    gy = vy * 8 + lane % EY - 1 + 64
    voxel = (((gx >> 1) & 15) * 8 + ((gy >> 3) & 7)) * 16 + (gx & 1) * 8 + (gy & 7)
    off_lane = lane & 15
    ej = lax.broadcasted_iota(I32, (128, PLANES * STRATUM), 0)
    ek = lax.broadcasted_iota(I32, (128, PLANES * STRATUM), 1)
    spread = jnp.where((ek >> 4) == ej, 1.0, 0.0).astype(BF16)
    scale = 1.0 / 512.0

    for g in range(RZ):
        bits = rc_ref[:, g : g + 1] & voxel
        for s in (8, 4, 2, 1):
            bits = bits ^ (bits >> s)
        sgn = (1 - 2 * (bits & 1)).astype(F32).astype(BF16)
        wide = jnp.dot(sgn, spread, preferred_element_type=F32)
        pick = so_ref[:, g : g + 1] == off_lane
        parts = [
            jnp.where(pick, wide[:, k * 128 : (k + 1) * 128], 0.0).astype(BF16)
            for k in range(PLANES * STRATUM // 128)
        ]
        s_mat = jnp.concatenate(parts, axis=1)
        c = jnp.dot(s_mat, tt_hi[g], preferred_element_type=F32)
        c = c + jnp.dot(s_mat, tt_lo[g], preferred_element_type=F32)
        c_ref[g] = (c * scale).reshape(RY, RX, KD, COLS)


def contributions(vol, ext, rc, so):
    return pl.pallas_call(
        local_kernel,
        out_shape=jax.ShapeDtypeStruct((RZ, RY, RX, KD, COLS), F32),
        in_specs=[pl.BlockSpec(memory_space=pltpu.VMEM)] * 4,
        out_specs=pl.BlockSpec(memory_space=pltpu.VMEM),
        scratch_shapes=[
            pltpu.VMEM((COLS * 16, 128), F32),
            pltpu.VMEM((EX, EY + 2, COLS, 128), F32),
            pltpu.VMEM((RZ, PLANES * STRATUM, COLS), BF16),
            pltpu.VMEM((RZ, PLANES * STRATUM, COLS), BF16),
        ],
        compiler_params=pltpu.CompilerParams(vmem_limit_bytes=60 * 1024 * 1024),
        name="contributions",
    )(vol, ext, rc, so)


def comm_kernel(
    order_ref, c_ref, sk_ref, gram_ref,
    c, ra1, ra2, rb1, rb2, rz, other, gs, r1, p1, r2, p3, out,
    ld_sem, a_send, a_recv, z_send, z_recv, g_send, g_recv,
):
    vx, vy, sj = lax.axis_index("vx"), lax.axis_index("vy"), lax.axis_index("subj")
    x, y = lax.rem(vx, RX), lax.div(vx, RX)

    def xy(dx, dy):
        return (lax.rem(y + dy + RY, RY) * RX + lax.rem(x + dx + RX, RX), vy, sj)

    def plane_dev(o):
        return (lax.rem(vx + o, PLANE), vy, sj)

    def z_dev(o):
        return (vx, lax.rem(vy + o, RZ), sj)

    partner = (vx, vy, 1 - sj)
    barrier = pltpu.get_barrier_semaphore()
    peers = [plane_dev(o) for o in range(1, PLANE)] + [z_dev(o) for o in range(1, RZ)] + [partner]
    for d in peers:
        pl.semaphore_signal(barrier, inc=1, device_id=d, device_id_type=MESH)

    load = pltpu.make_async_copy(c_ref, c, ld_sem)
    load.start()

    lanes = lax.broadcasted_iota(I32, (64, 512), 1)
    rows = lax.broadcasted_iota(I32, (64, 512), 0)
    mover = jnp.concatenate(
        [jnp.where(lanes == order_ref[s] * 64 + rows, 1.0, 0.0).astype(BF16) for s in range(8)], axis=0
    )
    load.wait()
    pl.semaphore_wait(barrier, len(peers))

    def remote(src, dst, ssem, rsem, dev):
        return pltpu.make_async_remote_copy(
            src_ref=src, dst_ref=dst, send_sem=ssem, recv_sem=rsem, device_id=dev, device_id_type=MESH
        )

    started = []

    def go(copy):
        copy.start()
        started.append(copy)
        return copy

    lanes_of = [pl.ds(0, HALF), pl.ds(HALF, HALF)]
    x1, x2, x3 = lax.rem(x + 1, RX), lax.rem(x + 2, RX), lax.rem(x + 3, RX)
    y1, y2, y3 = lax.rem(y + 1, RY), lax.rem(y + 2, RY), lax.rem(y + 3, RY)
    A1, A2, B1, B2 = {}, {}, {}, {}

    def sems(g, h, k):
        return a_send.at[g, h, k], a_recv.at[g, h, k]

    def start_a1(g):
        for h in range(2):
            L = lanes_of[h]
            for k in range(2):
                cross = pl.ds(2 * k, 2)
                if h == 0:
                    src, dev = c.at[g, cross, x2, :, L], xy(1 - 2 * k, 0)
                else:
                    src, dev = c.at[g, y2, cross, :, L], xy(0, 1 - 2 * k)
                A1[g, h, k] = go(remote(src, ra1.at[g, h, k], *sems(g, h, k), dev))

    def do_a2(g):
        for h in range(2):
            L = lanes_of[h]
            for k in range(2):
                A1[g, h, k].wait_recv()
                cross = pl.ds(2 * k, 2)
                if h == 0:
                    nxt = (x1, x3)[k]
                    c[g, cross, nxt, :, L] = c[g, cross, nxt, :, L] + ra1[g, h, k]
                    src, dev = c.at[g, :, nxt, :, L], xy(1 - 2 * k, 0)
                else:
                    nxt = (y1, y3)[k]
                    c[g, nxt, cross, :, L] = c[g, nxt, cross, :, L] + ra1[g, h, k]
                    src, dev = c.at[g, nxt, :, :, L], xy(0, 1 - 2 * k)
                A2[g, h, k] = go(remote(src, ra2.at[g, h, k], *sems(g, h, 2 + k), dev))

    def do_b1(g):
        for h in range(2):
            L = lanes_of[h]
            A2[g, h, 0].wait_recv()
            A2[g, h, 1].wait_recv()
            if h == 0:
                c[g, :, x, :, L] = c[g, :, x, :, L] + ra2[g, h, 0] + ra2[g, h, 1]
            else:
                c[g, y, :, :, L] = c[g, y, :, :, L] + ra2[g, h, 0] + ra2[g, h, 1]
            for k in range(2):
                part = pl.ds(16 * k, 16)
                if h == 0:
                    src, dev = c.at[g, y2, x, part, L], xy(0, 1 - 2 * k)
                else:
                    src, dev = c.at[g, y, x2, part, L], xy(1 - 2 * k, 0)
                B1[g, h, k] = go(remote(src, rb1.at[g, h, k], *sems(g, h, 4 + k), dev))

    def do_b2(g):
        for h in range(2):
            L = lanes_of[h]
            for k in range(2):
                B1[g, h, k].wait_recv()
                part = pl.ds(16 * k, 16)
                if h == 0:
                    nxt = (y1, y3)[k]
                    c[g, nxt, x, part, L] = c[g, nxt, x, part, L] + rb1[g, h, k]
                    src, dev = c.at[g, nxt, x, :, L], xy(0, 1 - 2 * k)
                else:
                    nxt = (x1, x3)[k]
                    c[g, y, nxt, part, L] = c[g, y, nxt, part, L] + rb1[g, h, k]
                    src, dev = c.at[g, y, nxt, :, L], xy(1 - 2 * k, 0)
                B2[g, h, k] = go(remote(src, rb2.at[g, h, k], *sems(g, h, 6 + k), dev))

    def do_b3(g):
        for h in range(2):
            L = lanes_of[h]
            B2[g, h, 0].wait_recv()
            B2[g, h, 1].wait_recv()
            c[g, y, x, :, L] = c[g, y, x, :, L] + rb2[g, h, 0] + rb2[g, h, 1]

    for g in range(RZ):
        start_a1(g)
    for g in range(2):
        do_a2(g)
    for g in range(RZ + 4):
        if g + 2 < RZ:
            do_a2(g + 2)
        if g < RZ:
            do_b1(g)
        if 0 <= g - 2 < RZ:
            do_b2(g - 2)
        if 0 <= g - 4 < RZ:
            do_b3(g - 4)

    zc = []
    for o in range(1, RZ):
        g = lax.rem(vy + o, RZ)
        zc.append(go(remote(c.at[g, y, x], rz.at[o - 1], z_send.at[o - 1], z_recv.at[o - 1], z_dev(o))))
    total = c[vy, y, x]
    for o in range(1, RZ):
        zc[o - 1].wait_recv()
        total = total + rz[o - 1]
    sk_ref[...] = total

    swap = go(remote(sk_ref, other, z_send.at[7], z_recv.at[7], partner))
    swap.wait_recv()
    theirs = other[...]
    first = jnp.where(sj == 0, 1.0, 0.0)
    left = total * first + theirs * (1.0 - first)
    right = theirs * first + total * (1.0 - first)
    parts = jnp.concatenate(split2(jnp.concatenate([left, right], axis=1)), axis=0)
    moved = jnp.dot(parts, mover, preferred_element_type=F32)
    mine = moved[:, :COLS] * first + moved[:, COLS:] * (1.0 - first)
    lhs = jnp.concatenate([mine[:KD], mine[:KD], mine[KD:]], axis=0).astype(BF16)
    rhs = jnp.concatenate([moved[:KD], moved[KD:], moved[:KD]], axis=0).astype(BF16)
    part = lax.dot_general(lhs, rhs, (((0,), (0,)), ((), ())), preferred_element_type=F32)
    for i in range(32):
        for j in range(4):
            gs[4 * i + j] = part[8 * i : 8 * i + 8, 128 * j : 128 * j + 128]

    cp = []
    for o in range(1, PLANE):
        d = lax.rem(vx + o, PLANE)
        cp.append(go(remote(gs.at[pl.ds(d * 8, 8)], r1.at[o - 1], g_send.at[0, o], g_recv.at[0, o], plane_dev(o))))
    acc = gs[pl.ds(vx * 8, 8)]
    for o in range(1, PLANE):
        cp[o - 1].wait_recv()
        acc = acc + r1[o - 1]
    p1[...] = acc
    cp = []
    for o in range(1, RZ):
        d = lax.rem(vy + o, RZ)
        cp.append(go(remote(p1.at[d], r2.at[o - 1], g_send.at[1, o], g_recv.at[1, o], z_dev(o))))
    acc = p1[vy]
    for o in range(1, RZ):
        cp[o - 1].wait_recv()
        acc = acc + r2[o - 1]
    p3[vy] = acc * (1.0 / 4096.0)
    cp = []
    for o in range(1, RZ):
        cp.append(go(remote(p3.at[vy], p3.at[vy], g_send.at[2, o], g_recv.at[2, o], z_dev(o))))
    for o in range(1, RZ):
        cp[o - 1].wait_recv()
    cp = []
    for o in range(1, PLANE):
        cp.append(go(remote(p3, out.at[pl.ds(vx * 8, 8)], g_send.at[3, o], g_recv.at[3, o], plane_dev(o))))
    out[pl.ds(vx * 8, 8)] = p3[...]
    for o in range(1, PLANE):
        cp[o - 1].wait_recv()
    for i in range(32):
        for j in range(4):
            gram_ref[8 * i : 8 * i + 8, 128 * j : 128 * j + 128] = out[4 * i + j]
    for copy in started:
        copy.wait_send()


def reduce_and_gram(order, c):
    V = pltpu.VMEM
    dma = pltpu.SemaphoreType.DMA
    return pl.pallas_call(
        comm_kernel,
        out_shape=(
            jax.ShapeDtypeStruct((KD, COLS), F32),
            jax.ShapeDtypeStruct((COLS, 2 * COLS), F32),
        ),
        in_specs=[pl.BlockSpec(memory_space=pltpu.SMEM), pl.BlockSpec(memory_space=pl.ANY)],
        out_specs=(pl.BlockSpec(memory_space=V), pl.BlockSpec(memory_space=V)),
        scratch_shapes=[
            V((RZ, RY, RX, KD, COLS), F32),
            V((RZ, 2, 2, 2, KD, HALF), F32),
            V((RZ, 2, 2, 4, KD, HALF), F32),
            V((RZ, 2, 2, KD // 2, HALF), F32),
            V((RZ, 2, 2, KD, HALF), F32),
            V((RZ - 1, KD, COLS), F32),
            V((KD, COLS), F32),
            V((128, 8, 128), F32),
            V((PLANE - 1, 8, 8, 128), F32),
            V((8, 8, 128), F32),
            V((RZ - 1, 8, 128), F32),
            V((8, 8, 128), F32),
            V((128, 8, 128), F32),
            dma,
            dma((RZ, 2, 8)),
            dma((RZ, 2, 8)),
            dma((8,)),
            dma((8,)),
            dma((4, 16)),
            dma((4, 16)),
        ],
        compiler_params=pltpu.CompilerParams(
            collective_id=1, has_side_effects=True, vmem_limit_bytes=40 * 1024 * 1024
        ),
        name="reduce_and_gram",
    )(order, c)


def on_device(volumes, flip_bits, hadamard_block, stratum_offset, subject_order):
    vol = volumes.reshape(COLS * 2, 8, 128)
    ext = sign_halo(flip_bits)
    block = hadamard_block.reshape(PLANE, RZ, KD)
    rc = (block * 16 + jnp.arange(PLANE, dtype=I32)[:, None, None]).transpose(0, 2, 1).reshape(PLANE * KD, RZ)
    so = stratum_offset.reshape(PLANE, RZ, KD).transpose(0, 2, 1).reshape(PLANE * KD, RZ)
    c = contributions(vol, ext, rc, so)
    return reduce_and_gram(subject_order, c)


def solution(mesh):
    placed = (P("subj", None, "vx", "vy", None), P("vx", "vy", None), P(), P(), P())
    return jax.shard_map(
        on_device,
        mesh=mesh,
        in_specs=placed,
        out_specs=(P(("vx", "vy"), "subj"), P("subj", None)),
        check_vma=False,
    )
```

time: 357 us -> 107 us (0.30); the launches traced: 352 us -> 106 us
  waiting for transfers between devices: 273 us -> 0 us
  Pallas kernels: 0 us -> 98.6 us
  starting transfers between devices: 27.5 us -> 0 us
  matrix products: 15.7 us -> 0 us
  between operations: 14.3 us -> 0.66 us
  other arithmetic: 8.81 us -> 0.74 us
  blocking collectives: 6.47 us -> 0 us
    psum x1 -> x0, waiting for transfers between devices: 207 us -> none  [on_device(): gram_block = lax.psum(partial_gram, ('vx', 'vy')) / (KD * groups)]
    pallas_call x0 -> x3, Pallas kernels: none -> 98.6 us  [the longest x1 68.4 us: reduce_and_gram(): pl.pallas_call(comm_kernel, out_shape=(jax.ShapeDtypeStruct((KD, COLS), F...]
    all_to_all x1 -> x0, waiting for transfers between devices: 47.3 us -> none  [on_device(): lax.all_to_all(mixed_rows.reshape(block_width, groups, stratum), ('vx', '...]
    ppermute x4 -> x0, waiting for transfers between devices: 19 us -> none  [the longest x2 11.6 us: padded_2(): lax.ppermute(tail, axis, [(i, (i + 1) % count) for i in range(ends)])]
    all_to_all x1 -> x0, starting transfers between devices: 17.4 us -> none  [on_device(): lax.all_to_all(mixed_rows.reshape(block_width, groups, stratum), ('vx', '...]
    dot_general x6 -> x0, matrix products: 15.7 us -> none  [the longest x1 5.96 us: on_device(): jnp.einsum('crd,rd->rc', picked, block_signs, precision=highest_level)]
    ppermute x4 -> x0, starting transfers between devices: 10.1 us -> none  [the longest x2 7.52 us: padded_2(): lax.ppermute(tail, axis, [(i, (i + 1) % count) for i in range(ends)])]
    all_gather x1 -> x0, blocking collectives: 6.47 us -> none  [on_device(): whole = lax.all_gather(sketch_block, 'subj', axis=1, tiled=True)]
  transfers between devices with their start and end apart: 6 -> 0, of which waited for: 6 -> 0; matrix products, arithmetic and copies ran while one was open for 1% -> 0% of each run, Pallas kernels for 0% -> 0%
where the time goes in v1:
time: 107 us; the launch traced here: 106 us
  Pallas kernels  98.6 us (92%)
  local copies, waits for them, and re-layouts  6.14 us (6%)
    pallas_call x1, Pallas kernels, reduce_and_gram(): pl.pallas_call(comm_kernel, out_shape=(jax.ShapeDtypeStruct((KD, COLS), F...  68.4 us
    pallas_call x1, Pallas kernels, contributions(): pl.pallas_call(local_kernel, out_shape=jax.ShapeDtypeStruct((RZ, RY, RX,...  15.5 us
    pallas_call x1, Pallas kernels, sign_halo(): pl.pallas_call(halo_kernel, out_shape=jax.ShapeDtypeStruct((EX, EY, 1, 12...  14.7 us
    unnamed x6, local copies, waits for them, and re-layouts  3.6 us

profile of v1, /device:TPU:1, one launch (start us, length us, event | category | flops | bytes accessed | tf_op | source)
XLA Modules:
  0.0 106.1 jit_solution(8466210943703984676)
XLA Ops:
  0.6 0.0 copy-start.1
  0.6 0.7 broadcast_multiply_fusion
  1.4 14.7 %sign_halo.1.ext_ref = f32[4,10,1,128]{3,2,1,0:T(1,128)} custom-call(s32[2,8,128]{2,1,0:T(8,128)} %flip_ref.1), custom_call_target="tpu_custom_call" | custom-call | tf_op jit(solution)/shard_map/sign_halo/pallas_call | solution.py:79
  16.1 0.1 mul.11
  16.2 0.8 reshape.21
  17.0 0.8 copy.8
  17.8 0.8 copy.7
  18.6 15.5 %contributions.1.c_ref = f32[8,4,4,32,256]{4,3,2,1,0:T(8,128)} custom-call(bf16[512,8,128]{2,1,0:T(8,128)(2,1)} %bitcast.6, f32[4,10,1,128]{3,2,1,0:T(1,128)} %sign_halo.1.ext_ref, s32[512,8]{1,0:T(8,128)} %bitcast.8, s32[512,8]{1,0:T(8,128)} %bitcast.7), custom_call_target="tpu_custom_call" | custom-call | tf_op jit(solution)/shard_map/contributions/pallas_call | solution.py:172
  34.1 0.0 copy-done.1
  34.1 0.0 copy-start
  34.1 2.2 %copy-done = f32[8,4,4,32,256]{4,3,2,1,0:T(8,128)S(1)} copy-done((f32[8,4,4,32,256]{4,3,2,1,0:T(8,128)S(1)}, f32[8,4,4,32,256]{4,3,2,1,0:T(8,128)}, u32[]{:S(2)}) %copy-start) | copy-done | bytes 4194328
  36.3 68.4 %reduce_and_gram.1 = (f32[32,256]{1,0:T(8,128)S(1)}, f32[256,512]{1,0:T(8,128)S(1)}) custom-call(s32[8]{0:T(128)S(1)} %copy-done.1, f32[8,4,4,32,256]{4,3,2,1,0:T(8,128)S(1)} %copy-done), custom_call_target="tpu_custom_call" | custom-call | tf_op jit(solution)/shard_map/reduce_and_gram/pallas_call | solution.py:388
  104.7 0.6 copy.11
  105.3 0.8 copy.12
  (1 shorter events, 0.0 us)
Async XLA Ops:
  0.6 33.5 %copy-start.1 = (s32[8]{0:T(128)S(1)}, s32[8]{0:T(128)}, u32[]{:S(2)}) copy-start(s32[8]{0:T(128)} %order_ref.1) | copy-start | bytes 100
  34.1 2.2 %copy-start = (f32[8,4,4,32,256]{4,3,2,1,0:T(8,128)S(1)}, f32[8,4,4,32,256]{4,3,2,1,0:T(8,128)}, u32[]{:S(2)}) copy-start(f32[8,4,4,32,256]{4,3,2,1,0:T(8,128)} %contributions.1.c_ref) | copy-start | bytes 12582916

commit v2 on v1

v2 whole, which is shorter than its diff:
```python
import jax
import jax.numpy as jnp
from jax import lax
from jax.experimental import pallas as pl
from jax.experimental.pallas import tpu as pltpu
from jax.sharding import PartitionSpec as P

MESH = pl.DeviceIdType.MESH
F32, BF16, I32 = jnp.float32, jnp.bfloat16, jnp.int32

w_side = 0.2741
w_mid = 0.4518

RX, RY, RZ = 4, 4, 8
PLANE = RX * RY
KD = 32
COLS = 256
HALF = 128
EX, EY = 4, 10
PLANES = EX * EY
STRATUM = 16


def split2(v):
    hi = v.astype(BF16)
    return hi, (v - hi.astype(F32)).astype(BF16)

HALO = [(dx, dy) for dx in (-1, 0, 1) for dy in (-1, 0, 1) if (dx, dy) != (0, 0)]
ORDER = (4, 3, 5, 2, 6, 1, 7, 0)
CHUNKS = 4
LAG_A2, LAG_B1, LAG_B2, LAG_B3 = 3, 5, 7, 9
BANDS = PLANES * STRATUM // 128


def parity_sign(bits, shifts):
    for s in shifts:
        bits = bits ^ (bits >> s)
    return jnp.where((bits & 1) == 0, 1.0, -1.0)


def kernel(
    order_ref, vol_hbm, flip_ref, block_ref, offset_ref, sk_ref, gram_ref,
    vol, halo, ext, codes, mover, zs, xs, tt_hi, tt_lo,
    c, ra1, ra2, rb1, rb2, rz, other, gs, r1, p1, r2, p3, out,
    ld_sem, h_send, h_recv, a_send, a_recv, z_send, z_recv, g_send, g_recv,
):
    vx, vy, sj = lax.axis_index("vx"), lax.axis_index("vy"), lax.axis_index("subj")
    x, y = lax.rem(vx, RX), lax.div(vx, RX)

    def xy(dx, dy):
        return (lax.rem(y + dy + RY, RY) * RX + lax.rem(x + dx + RX, RX), vy, sj)

    def plane_dev(o):
        return (lax.rem(vx + o, PLANE), vy, sj)

    def z_dev(o):
        return (vx, lax.rem(vy + o, RZ), sj)

    def near(dx, dy):
        return (lax.rem(vx + dx + PLANE, PLANE), lax.rem(vy + dy + RZ, RZ), sj)

    partner = (vx, vy, 1 - sj)

    loads = []
    per = COLS * 2 // CHUNKS
    for i in range(CHUNKS):
        part = pl.ds(i * per, per)
        loads.append(pltpu.make_async_copy(vol_hbm.at[part], vol.at[part], ld_sem.at[i]))
        loads[-1].start()

    barrier = pltpu.get_barrier_semaphore()
    peers = [plane_dev(o) for o in range(1, PLANE)] + [z_dev(o) for o in range(1, RZ)] + [partner]
    peers += [near(dx, dy) for dx, dy in HALO if dx * dy != 0]
    for d in peers:
        pl.semaphore_signal(barrier, inc=1, device_id=d, device_id_type=MESH)

    for bx in range(2):
        for by in range(8):
            ext[bx + 1, by + 1] = (2 * flip_ref[bx, pl.ds(by, 1), :] - 1).astype(F32)

    row = lax.broadcasted_iota(I32, (128, 128), 0)
    col = lax.broadcasted_iota(I32, (128, 128), 1)
    dist = jnp.abs(row - col)
    band = jnp.where(dist == 0, w_mid, jnp.where(dist == 1, w_side, 0.0)).astype(F32)
    wcat = jnp.concatenate(split2(band), axis=1)
    hz = parity_sign(row & col, (4, 2, 1)).astype(BF16)
    hcat = jnp.concatenate([hz, hz], axis=1)

    def smooth_z(i, _):
        v = vol[pl.ds(i * 32, 32)].astype(F32).reshape(256, 128).astype(BF16)
        r = jnp.dot(v, wcat, preferred_element_type=F32)
        zs[pl.ds(i * 256, 256), :] = r[:, :128] + r[:, 128:]
        return 0

    for i in range(CHUNKS):
        loads[i].wait()
        lax.fori_loop(i * per // 32, (i + 1) * per // 32, smooth_z, 0)

    def remote(src, dst, ssem, rsem, dev):
        return pltpu.make_async_remote_copy(
            src_ref=src, dst_ref=dst, send_sem=ssem, recv_sem=rsem, device_id=dev, device_id_type=MESH
        )

    started = []

    def go(copy):
        copy.start()
        started.append(copy)
        return copy

    pl.semaphore_wait(barrier, len(peers))
    signs = [
        go(remote(flip_ref, halo.at[i], h_send.at[i], h_recv.at[i], near(dx, dy)))
        for i, (dx, dy) in enumerate(HALO)
    ]

    zero = jnp.zeros((COLS, 128), F32)
    for ex in range(EX):
        for yi in (0, 1, 10, 11):
            xs[ex, yi] = zero
    for yi in range(8):
        a = zs[pl.ds(yi, COLS, stride=16), :]
        b = zs[pl.ds(8 + yi, COLS, stride=16), :]
        xs[0, yi + 2] = w_side * a
        xs[1, yi + 2] = w_mid * a + w_side * b
        xs[2, yi + 2] = w_side * a + w_mid * b
        xs[3, yi + 2] = w_side * b

    def plane(ex, yi):
        f = w_side * (xs[ex, yi] + xs[ex, yi + 2]) + w_mid * xs[ex, yi + 1]
        f = f * ext[ex, yi]
        fcat = jnp.concatenate(split2(f), axis=1)
        t = lax.dot_general(hcat, fcat, (((1,), (1,)), ((), ())), preferred_element_type=F32)
        thi, tlo = split2(t)
        at = pl.ds(pl.multiple_of((ex * EY + yi) * STRATUM, STRATUM), STRATUM)
        for g in range(RZ):
            tt_hi[g, at, :] = thi[g * STRATUM : (g + 1) * STRATUM, :]
            tt_lo[g, at, :] = tlo[g * STRATUM : (g + 1) * STRATUM, :]

    def own_planes(i, _):
        plane(1, i + 1)
        plane(2, i + 1)
        return 0

    lax.fori_loop(0, 8, own_planes, 0)

    code_t = (block_ref[...] * 16 + offset_ref[...]).astype(F32).T.astype(I32)
    for g in range(RZ):
        for p in range(PLANE):
            i = 2 * p + g // 4
            codes[g, p * KD : (p + 1) * KD, :] = jnp.broadcast_to(
                code_t[(g % 4) * KD : (g % 4 + 1) * KD, i : i + 1], (KD, 128)
            )

    lanes = lax.broadcasted_iota(I32, (64, 512), 1)
    rows = lax.broadcasted_iota(I32, (64, 512), 0)
    for s in range(8):
        mover[64 * s : 64 * s + 64, :] = jnp.where(lanes == order_ref[s] * 64 + rows, 1.0, 0.0).astype(BF16)

    okx = {-1: jnp.where(vx > 0, 1, 0), 0: 1, 1: jnp.where(vx < PLANE - 1, 1, 0)}
    oky = {-1: jnp.where(vy > 0, 1, 0), 0: 1, 1: jnp.where(vy < RZ - 1, 1, 0)}
    for copy in signs:
        copy.wait_recv()
    for i, (dx, dy) in enumerate(HALO):
        ok = (okx[-dx] * oky[-dy]).astype(F32)
        xpos = {-1: [(0, 1)], 0: [(1, 0), (2, 1)], 1: [(3, 0)]}[-dx]
        ypos = {-1: [(0, 7)], 0: [(k + 1, k) for k in range(8)], 1: [(9, 0)]}[-dy]
        for ex, bx in xpos:
            for ey, by in ypos:
                ext[ex, ey] = (2 * halo[i, bx, pl.ds(by, 1), :] - 1).astype(F32) * ok

    def x_planes(i, _):
        plane(0, i)
        plane(3, i)
        return 0

    def y_planes(i, _):
        plane(1, i * 9)
        plane(2, i * 9)
        return 0

    lax.fori_loop(0, EY, x_planes, 0)
    lax.fori_loop(0, 2, y_planes, 0)

    lane = lax.broadcasted_iota(I32, (1, 128), 1)
    gx = vx * 2 + lane // EY - 1 + 32
    gy = vy * 8 + lane % EY - 1 + 64
    voxel = (((gx >> 1) & 15) * 8 + ((gy >> 3) & 7)) * 16 + (gx & 1) * 8 + (gy & 7)
    off_lane = lane & 15
    ej = lax.broadcasted_iota(I32, (128, PLANES * STRATUM), 0)
    ek = lax.broadcasted_iota(I32, (128, PLANES * STRATUM), 1)
    spread = jnp.where((ek >> 4) == ej, 1.0, 0.0).astype(BF16)
    place = lax.broadcasted_iota(I32, (PLANE * KD, 128), 0) // KD

    def group(o):
        return lax.rem(vy + o, RZ)

    def contribute(o):
        g = group(o)
        code = codes[g]
        sgn = parity_sign(((code & -16) + place) & voxel, (8, 4, 2, 1)).astype(BF16)
        wide = jnp.dot(sgn, spread, preferred_element_type=F32)
        pick = (code & 15) == off_lane
        s_mat = jnp.concatenate(
            [jnp.where(pick, wide[:, k * 128 : (k + 1) * 128], 0.0).astype(BF16) for k in range(BANDS)], axis=1
        )
        r = jnp.dot(s_mat, tt_hi[g], preferred_element_type=F32)
        r = r + jnp.dot(s_mat, tt_lo[g], preferred_element_type=F32)
        c[g] = (r * (1.0 / 512.0)).reshape(RY, RX, KD, COLS)

    lanes_of = [pl.ds(0, HALF), pl.ds(HALF, HALF)]
    x1, x2, x3 = lax.rem(x + 1, RX), lax.rem(x + 2, RX), lax.rem(x + 3, RX)
    y1, y2, y3 = lax.rem(y + 1, RY), lax.rem(y + 2, RY), lax.rem(y + 3, RY)
    A1, A2, B1, B2, ZC = {}, {}, {}, {}, {}

    def sems(o, h, k):
        return a_send.at[o, h, k], a_recv.at[o, h, k]

    def start_a1(o):
        g = group(o)
        for h in range(2):
            L = lanes_of[h]
            for k in range(2):
                cross = pl.ds(2 * k, 2)
                if h == 0:
                    src, dev = c.at[g, cross, x2, :, L], xy(1 - 2 * k, 0)
                else:
                    src, dev = c.at[g, y2, cross, :, L], xy(0, 1 - 2 * k)
                A1[o, h, k] = go(remote(src, ra1.at[o, h, k], *sems(o, h, k), dev))

    def do_a2(o):
        g = group(o)
        for h in range(2):
            L = lanes_of[h]
            for k in range(2):
                A1[o, h, k].wait_recv()
                cross = pl.ds(2 * k, 2)
                if h == 0:
                    nxt = (x1, x3)[k]
                    c[g, cross, nxt, :, L] = c[g, cross, nxt, :, L] + ra1[o, h, k]
                    src, dev = c.at[g, :, nxt, :, L], xy(1 - 2 * k, 0)
                else:
                    nxt = (y1, y3)[k]
                    c[g, nxt, cross, :, L] = c[g, nxt, cross, :, L] + ra1[o, h, k]
                    src, dev = c.at[g, nxt, :, :, L], xy(0, 1 - 2 * k)
                A2[o, h, k] = go(remote(src, ra2.at[o, h, k], *sems(o, h, 2 + k), dev))

    def do_b1(o):
        g = group(o)
        for h in range(2):
            L = lanes_of[h]
            A2[o, h, 0].wait_recv()
            A2[o, h, 1].wait_recv()
            if h == 0:
                c[g, :, x, :, L] = c[g, :, x, :, L] + ra2[o, h, 0] + ra2[o, h, 1]
            else:
                c[g, y, :, :, L] = c[g, y, :, :, L] + ra2[o, h, 0] + ra2[o, h, 1]
            for k in range(2):
                part = pl.ds(16 * k, 16)
                if h == 0:
                    src, dev = c.at[g, y2, x, part, L], xy(0, 1 - 2 * k)
                else:
                    src, dev = c.at[g, y, x2, part, L], xy(1 - 2 * k, 0)
                B1[o, h, k] = go(remote(src, rb1.at[o, h, k], *sems(o, h, 4 + k), dev))

    def do_b2(o):
        g = group(o)
        for h in range(2):
            L = lanes_of[h]
            for k in range(2):
                B1[o, h, k].wait_recv()
                part = pl.ds(16 * k, 16)
                if h == 0:
                    nxt = (y1, y3)[k]
                    c[g, nxt, x, part, L] = c[g, nxt, x, part, L] + rb1[o, h, k]
                    src, dev = c.at[g, nxt, x, :, L], xy(0, 1 - 2 * k)
                else:
                    nxt = (x1, x3)[k]
                    c[g, y, nxt, part, L] = c[g, y, nxt, part, L] + rb1[o, h, k]
                    src, dev = c.at[g, y, nxt, :, L], xy(1 - 2 * k, 0)
                B2[o, h, k] = go(remote(src, rb2.at[o, h, k], *sems(o, h, 6 + k), dev))

    def do_b3(o):
        g = group(o)
        for h in range(2):
            L = lanes_of[h]
            B2[o, h, 0].wait_recv()
            B2[o, h, 1].wait_recv()
            c[g, y, x, :, L] = c[g, y, x, :, L] + rb2[o, h, 0] + rb2[o, h, 1]
        if o:
            ZC[o] = go(remote(c.at[g, y, x], rz.at[o - 1], z_send.at[o - 1], z_recv.at[o - 1], z_dev(o)))

    stages = ((0, contribute), (0, start_a1), (LAG_A2, do_a2), (LAG_B1, do_b1), (LAG_B2, do_b2), (LAG_B3, do_b3))
    for step in range(RZ + LAG_B3):
        for lag, stage in stages:
            if 0 <= step - lag < RZ:
                stage(ORDER[step - lag])

    total = c[vy, y, x]
    for o in ORDER[:-1]:
        ZC[o].wait_recv()
        total = total + rz[o - 1]
    sk_ref[...] = total

    swap = go(remote(sk_ref, other, z_send.at[7], z_recv.at[7], partner))
    swap.wait_recv()
    theirs = other[...]
    first = jnp.where(sj == 0, 1.0, 0.0)
    left = total * first + theirs * (1.0 - first)
    right = theirs * first + total * (1.0 - first)
    parts = jnp.concatenate(split2(jnp.concatenate([left, right], axis=1)), axis=0)
    moved = jnp.dot(parts, mover[...], preferred_element_type=F32)
    mine = moved[:, :COLS] * first + moved[:, COLS:] * (1.0 - first)
    lhs = jnp.concatenate([mine[:KD], mine[:KD], mine[KD:]], axis=0).astype(BF16)
    rhs = jnp.concatenate([moved[:KD], moved[KD:], moved[:KD]], axis=0).astype(BF16)
    part = lax.dot_general(lhs, rhs, (((0,), (0,)), ((), ())), preferred_element_type=F32)
    for i in range(32):
        for j in range(4):
            gs[4 * i + j] = part[8 * i : 8 * i + 8, 128 * j : 128 * j + 128]

    cp = []
    for o in range(1, PLANE):
        d = lax.rem(vx + o, PLANE)
        cp.append(go(remote(gs.at[pl.ds(d * 8, 8)], r1.at[o - 1], g_send.at[0, o], g_recv.at[0, o], plane_dev(o))))
    acc = gs[pl.ds(vx * 8, 8)]
    for o in range(1, PLANE):
        cp[o - 1].wait_recv()
        acc = acc + r1[o - 1]
    p1[...] = acc
    cp = []
    for o in range(1, RZ):
        d = lax.rem(vy + o, RZ)
        cp.append(go(remote(p1.at[d], r2.at[o - 1], g_send.at[1, o], g_recv.at[1, o], z_dev(o))))
    acc = p1[vy]
    for o in range(1, RZ):
        cp[o - 1].wait_recv()
        acc = acc + r2[o - 1]
    p3[vy] = acc * (1.0 / 4096.0)
    cp = []
    for o in range(1, RZ):
        cp.append(go(remote(p3.at[vy], p3.at[vy], g_send.at[2, o], g_recv.at[2, o], z_dev(o))))
    for o in range(1, RZ):
        cp[o - 1].wait_recv()
    cp = []
    for o in range(1, PLANE):
        cp.append(go(remote(p3, out.at[pl.ds(vx * 8, 8)], g_send.at[3, o], g_recv.at[3, o], plane_dev(o))))
    out[pl.ds(vx * 8, 8)] = p3[...]
    for o in range(1, PLANE):
        cp[o - 1].wait_recv()
    for i in range(32):
        for j in range(4):
            gram_ref[8 * i : 8 * i + 8, 128 * j : 128 * j + 128] = out[4 * i + j]
    for copy in started:
        copy.wait_send()


def sketch_and_gram(order, vol, flip, block, offset):
    V = pltpu.VMEM
    dma = pltpu.SemaphoreType.DMA
    return pl.pallas_call(
        kernel,
        out_shape=(
            jax.ShapeDtypeStruct((KD, COLS), F32),
            jax.ShapeDtypeStruct((COLS, 2 * COLS), F32),
        ),
        in_specs=[
            pl.BlockSpec(memory_space=pltpu.SMEM),
            pl.BlockSpec(memory_space=pl.ANY),
            pl.BlockSpec(memory_space=V),
            pl.BlockSpec(memory_space=V),
            pl.BlockSpec(memory_space=V),
        ],
        out_specs=(pl.BlockSpec(memory_space=V), pl.BlockSpec(memory_space=V)),
        scratch_shapes=[
            V((COLS * 2, 8, 128), BF16),
            V((8, 2, 8, 128), I32),
            V((EX, EY, 1, 128), F32),
            V((RZ, PLANE * KD, 128), I32),
            V((512, 512), BF16),
            V((COLS * 16, 128), F32),
            V((EX, EY + 2, COLS, 128), F32),
            V((RZ, PLANES * STRATUM, COLS), BF16),
            V((RZ, PLANES * STRATUM, COLS), BF16),
            V((RZ, RY, RX, KD, COLS), F32),
            V((RZ, 2, 2, 2, KD, HALF), F32),
            V((RZ, 2, 2, 4, KD, HALF), F32),
            V((RZ, 2, 2, KD // 2, HALF), F32),
            V((RZ, 2, 2, KD, HALF), F32),
            V((RZ - 1, KD, COLS), F32),
            V((KD, COLS), F32),
            V((128, 8, 128), F32),
            V((PLANE - 1, 8, 8, 128), F32),
            V((8, 8, 128), F32),
            V((RZ - 1, 8, 128), F32),
            V((8, 8, 128), F32),
            V((128, 8, 128), F32),
            dma((CHUNKS,)),
            dma((8,)),
            dma((8,)),
            dma((RZ, 2, 8)),
            dma((RZ, 2, 8)),
            dma((8,)),
            dma((8,)),
            dma((4, 16)),
            dma((4, 16)),
        ],
        compiler_params=pltpu.CompilerParams(
            collective_id=0, has_side_effects=True, vmem_limit_bytes=60 * 1024 * 1024
        ),
        name="sketch_and_gram",
    )(order, vol, flip, block, offset)


def on_device(volumes, flip_bits, hadamard_block, stratum_offset, subject_order):
    return sketch_and_gram(
        subject_order,
        volumes.reshape(COLS * 2, 8, 128),
        flip_bits,
        hadamard_block.reshape(32, 128),
        stratum_offset.reshape(32, 128),
    )


def solution(mesh):
    placed = (P("subj", None, "vx", "vy", None), P("vx", "vy", None), P(), P(), P())
    return jax.shard_map(
        on_device,
        mesh=mesh,
        in_specs=placed,
        out_specs=(P(("vx", "vy"), "subj"), P("subj", None)),
        check_vma=False,
    )
```

time: 107 us -> 86.6 us (0.81)
  Pallas kernels: 98.6 us -> 81.6 us
  local copies, waits for them, and re-layouts: 6.14 us -> 3.24 us
    pallas_call x3 -> x1, Pallas kernels: 98.6 us -> 81.6 us  [sketch_and_gram(): pl.pallas_call(kernel, out_shape=(jax.ShapeDtypeStruct((KD, COLS), F32),...]
    transpose x2 -> x0, local copies, waits for them, and re-layouts: 1.67 us -> none  [the longest x1 0.84 us: on_device(): (block * 16 + jnp.arange(PLANE, dtype=I32)[:, None, None]).transpose(0, 2...]
    unnamed x6 -> x2, local copies, waits for them, and re-layouts: 3.6 us -> 3.24 us
where the time goes in v2:
time: 86.6 us; the launch traced here: 85.5 us
  Pallas kernels  81.6 us (94%)
  local copies, waits for them, and re-layouts  3.24 us (4%)
    pallas_call x1, Pallas kernels, sketch_and_gram(): pl.pallas_call(kernel, out_shape=(jax.ShapeDtypeStruct((KD, COLS), F32),...  81.6 us
    unnamed x2, local copies, waits for them, and re-layouts  3.24 us

profile of v2, /device:TPU:1, one launch (start us, length us, event | category | flops | bytes accessed | tf_op | source)
XLA Modules:
  0.0 85.5 jit_solution(13425360405261229589)
XLA Ops:
  0.6 81.6 %sketch_and_gram.1 = (f32[32,256]{1,0:T(8,128)}, f32[256,512]{1,0:T(8,128)}) custom-call(s32[8]{0:T(128)} %order_ref.1, bf16[512,8,128]{2,1,0:T(8,128)(2,1)} %bitcast.3, s32[2,8,128]{2,1,0:T(8,128)} %flip_ref.1, s32[32,128]{1,0:T(8,128)} %bitcast.4, s32[32,128]{1,0:T(8,128)} %bitcast.5), custom_call_target="tpu_custom_call" | custom-call | tf_op jit(solution)/shard_map/sketch_and_gram/pallas_call | solution.py:360
  82.3 1.4 %copy.9 = f32[32,256]{1,0:T(8,128)} copy(f32[32,256]{1,0:T(8,128)} %get-tuple-element.4) | data formatting | bytes 65536
  83.6 1.9 %copy.10 = f32[256,512]{1,0:T(8,128)} copy(f32[256,512]{1,0:T(8,128)} %get-tuple-element.5) | data formatting | bytes 1048576

commit v3 on v2

--- a/solution.py
+++ b/solution.py
@@ -28,7 +28,9 @@
 HALO = [(dx, dy) for dx in (-1, 0, 1) for dy in (-1, 0, 1) if (dx, dy) != (0, 0)]
 ORDER = (4, 3, 5, 2, 6, 1, 7, 0)
 CHUNKS = 4
-LAG_A2, LAG_B1, LAG_B2, LAG_B3 = 3, 5, 7, 9
+LAG_A2, LAG_B1, LAG_B2, LAG_B3 = 3, 7, 9, 11
+ZR = 8
+XR = KD - ZR
 BANDS = PLANES * STRATUM // 128
 
 
@@ -41,8 +43,8 @@
 def kernel(
     order_ref, vol_hbm, flip_ref, block_ref, offset_ref, sk_ref, gram_ref,
     vol, halo, ext, codes, mover, zs, xs, tt_hi, tt_lo,
-    c, ra1, ra2, rb1, rb2, rz, other, gs, r1, p1, r2, p3, out,
-    ld_sem, h_send, h_recv, a_send, a_recv, z_send, z_recv, g_send, g_recv,
+    c, ra1, ra2, rb1, rb2, rz, rv, rw, other, gs, r1, p1, r2, p3, out,
+    ld_sem, h_send, h_recv, a_send, a_recv, z_send, z_recv, v_send, v_recv, g_send, g_recv,
 ):
     vx, vy, sj = lax.axis_index("vx"), lax.axis_index("vy"), lax.axis_index("subj")
     x, y = lax.rem(vx, RX), lax.div(vx, RX)
@@ -209,9 +211,10 @@
         c[g] = (r * (1.0 / 512.0)).reshape(RY, RX, KD, COLS)
 
     lanes_of = [pl.ds(0, HALF), pl.ds(HALF, HALF)]
+    X, ZF = pl.ds(ZR, XR), pl.ds(0, ZR)
     x1, x2, x3 = lax.rem(x + 1, RX), lax.rem(x + 2, RX), lax.rem(x + 3, RX)
     y1, y2, y3 = lax.rem(y + 1, RY), lax.rem(y + 2, RY), lax.rem(y + 3, RY)
-    A1, A2, B1, B2, ZC = {}, {}, {}, {}, {}
+    A1, A2, B1, B2, ZC, ZV, ZW = {}, {}, {}, {}, {}, {}, {}
 
     def sems(o, h, k):
         return a_send.at[o, h, k], a_recv.at[o, h, k]
@@ -223,9 +226,9 @@
             for k in range(2):
                 cross = pl.ds(2 * k, 2)
                 if h == 0:
-                    src, dev = c.at[g, cross, x2, :, L], xy(1 - 2 * k, 0)
+                    src, dev = c.at[g, cross, x2, X, L], xy(1 - 2 * k, 0)
                 else:
-                    src, dev = c.at[g, y2, cross, :, L], xy(0, 1 - 2 * k)
+                    src, dev = c.at[g, y2, cross, X, L], xy(0, 1 - 2 * k)
                 A1[o, h, k] = go(remote(src, ra1.at[o, h, k], *sems(o, h, k), dev))
 
     def do_a2(o):
@@ -237,13 +240,19 @@
                 cross = pl.ds(2 * k, 2)
                 if h == 0:
                     nxt = (x1, x3)[k]
-                    c[g, cross, nxt, :, L] = c[g, cross, nxt, :, L] + ra1[o, h, k]
-                    src, dev = c.at[g, :, nxt, :, L], xy(1 - 2 * k, 0)
+                    c[g, cross, nxt, X, L] = c[g, cross, nxt, X, L] + ra1[o, h, k]
+                    src, dev = c.at[g, :, nxt, X, L], xy(1 - 2 * k, 0)
                 else:
                     nxt = (y1, y3)[k]
-                    c[g, nxt, cross, :, L] = c[g, nxt, cross, :, L] + ra1[o, h, k]
-                    src, dev = c.at[g, nxt, :, :, L], xy(0, 1 - 2 * k)
+                    c[g, nxt, cross, X, L] = c[g, nxt, cross, X, L] + ra1[o, h, k]
+                    src, dev = c.at[g, nxt, :, X, L], xy(0, 1 - 2 * k)
                 A2[o, h, k] = go(remote(src, ra2.at[o, h, k], *sems(o, h, 2 + k), dev))
+
+    def far_rows(o, k):
+        return (pl.ds(ZR, 16), pl.ds(ZR + 16, XR - 16)) if o % 2 == 0 else (pl.ds(ZR + 8, 16), pl.ds(ZR, 8))
+
+    def far_buf(o, h, k):
+        return rb1.at[o, h, k, pl.ds(0, 16 - 8 * k)]
 
     def do_b1(o):
         g = group(o)
@@ -252,16 +261,17 @@
             A2[o, h, 0].wait_recv()
             A2[o, h, 1].wait_recv()
             if h == 0:
-                c[g, :, x, :, L] = c[g, :, x, :, L] + ra2[o, h, 0] + ra2[o, h, 1]
+                c[g, :, x, X, L] = c[g, :, x, X, L] + ra2[o, h, 0] + ra2[o, h, 1]
             else:
-                c[g, y, :, :, L] = c[g, y, :, :, L] + ra2[o, h, 0] + ra2[o, h, 1]
+                c[g, y, :, X, L] = c[g, y, :, X, L] + ra2[o, h, 0] + ra2[o, h, 1]
             for k in range(2):
-                part = pl.ds(16 * k, 16)
+                part = far_rows(o, k)[k]
+                way = (1 - 2 * k) * (1 if o % 2 == 0 else -1)
                 if h == 0:
-                    src, dev = c.at[g, y2, x, part, L], xy(0, 1 - 2 * k)
+                    src, dev = c.at[g, y2, x, part, L], xy(0, way)
                 else:
-                    src, dev = c.at[g, y, x2, part, L], xy(1 - 2 * k, 0)
-                B1[o, h, k] = go(remote(src, rb1.at[o, h, k], *sems(o, h, 4 + k), dev))
+                    src, dev = c.at[g, y, x2, part, L], xy(way, 0)
+                B1[o, h, k] = go(remote(src, far_buf(o, h, k), *sems(o, h, 4 + k), dev))
 
     def do_b2(o):
         g = group(o)
@@ -269,15 +279,18 @@
             L = lanes_of[h]
             for k in range(2):
                 B1[o, h, k].wait_recv()
-                part = pl.ds(16 * k, 16)
+                part = far_rows(o, k)[k]
+                way = (1 - 2 * k) * (1 if o % 2 == 0 else -1)
+                at = 0 if way == 1 else 1
+                got = rb1[o, h, k, pl.ds(0, 16 - 8 * k)]
                 if h == 0:
-                    nxt = (y1, y3)[k]
-                    c[g, nxt, x, part, L] = c[g, nxt, x, part, L] + rb1[o, h, k]
-                    src, dev = c.at[g, nxt, x, :, L], xy(0, 1 - 2 * k)
+                    nxt = (y1, y3)[at]
+                    c[g, nxt, x, part, L] = c[g, nxt, x, part, L] + got
+                    src, dev = c.at[g, nxt, x, X, L], xy(0, way)
                 else:
-                    nxt = (x1, x3)[k]
-                    c[g, y, nxt, part, L] = c[g, y, nxt, part, L] + rb1[o, h, k]
-                    src, dev = c.at[g, y, nxt, :, L], xy(1 - 2 * k, 0)
+                    nxt = (x1, x3)[at]
+                    c[g, y, nxt, part, L] = c[g, y, nxt, part, L] + got
+                    src, dev = c.at[g, y, nxt, X, L], xy(way, 0)
                 B2[o, h, k] = go(remote(src, rb2.at[o, h, k], *sems(o, h, 6 + k), dev))
 
     def do_b3(o):
@@ -286,20 +299,60 @@
             L = lanes_of[h]
             B2[o, h, 0].wait_recv()
             B2[o, h, 1].wait_recv()
-            c[g, y, x, :, L] = c[g, y, x, :, L] + rb2[o, h, 0] + rb2[o, h, 1]
+            c[g, y, x, X, L] = c[g, y, x, X, L] + rb2[o, h, 0] + rb2[o, h, 1]
         if o:
-            ZC[o] = go(remote(c.at[g, y, x], rz.at[o - 1], z_send.at[o - 1], z_recv.at[o - 1], z_dev(o)))
+            ZC[o] = go(remote(c.at[g, y, x, X], rz.at[o - 1], z_send.at[o - 1], z_recv.at[o - 1], z_dev(o)))
+
+    def ring(n):
+        for k in range(2):
+            if n > 1:
+                ZV[n - 1, k].wait_recv()
+            to = group((4 - n + 1) if k == 0 else (4 + n - 1))
+            up = z_dev(1 if k == 0 else RZ - 1)
+            if n == 1:
+                half = pl.ds(2 * k, 2)
+                src, dst = c.at[to, half, :, ZF], rv.at[0, k, pl.ds(0, 2)]
+            else:
+                if n == 2:
+                    half = pl.ds(2 * k, 2)
+                    c[to, half, :, ZF] = c[to, half, :, ZF] + rv[0, k, pl.ds(0, 2)]
+                else:
+                    c[to, :, :, ZF] = c[to, :, :, ZF] + rv[n - 2, k]
+                src, dst = c.at[to, :, :, ZF], rv.at[n - 1, k]
+            ZV[n, k] = go(remote(src, dst, v_send.at[0, 2 * n - 2 + k], v_recv.at[0, 2 * n - 2 + k], up))
+
+    def spread_plane():
+        ZV[4, 0].wait_recv()
+        ZV[4, 1].wait_recv()
+        c[vy, :, :, ZF] = c[vy, :, :, ZF] + rv[3, 0] + rv[3, 1]
+        for o in range(1, PLANE):
+            d = lax.rem(vx + o, PLANE)
+            src = c.at[vy, lax.div(d, RX), lax.rem(d, RX), ZF]
+            ZW[o] = go(remote(src, rw.at[o - 1], v_send.at[1, o], v_recv.at[1, o], plane_dev(o)))
 
     stages = ((0, contribute), (0, start_a1), (LAG_A2, do_a2), (LAG_B1, do_b1), (LAG_B2, do_b2), (LAG_B3, do_b3))
+    ring_at = {0: 1, 3: 2, 6: 3, 8: 4}
     for step in range(RZ + LAG_B3):
-        for lag, stage in stages:
+        for lag, stage in stages[:2]:
             if 0 <= step - lag < RZ:
                 stage(ORDER[step - lag])
-
-    total = c[vy, y, x]
+        if step in ring_at:
+            ring(ring_at[step])
+        if step == 10:
+            spread_plane()
+        for lag, stage in stages[2:]:
+            if 0 <= step - lag < RZ:
+                stage(ORDER[step - lag])
+
+    low = c[vy, y, x, ZF]
+    for o in range(1, PLANE):
+        ZW[o].wait_recv()
+        low = low + rw[o - 1]
+    high = c[vy, y, x, X]
     for o in ORDER[:-1]:
         ZC[o].wait_recv()
-        total = total + rz[o - 1]
+        high = high + rz[o - 1]
+    total = jnp.concatenate([low, high], axis=0)
     sk_ref[...] = total
 
     swap = go(remote(sk_ref, other, z_send.at[7], z_recv.at[7], partner))
@@ -382,11 +435,13 @@
             V((RZ, PLANES * STRATUM, COLS), BF16),
             V((RZ, PLANES * STRATUM, COLS), BF16),
             V((RZ, RY, RX, KD, COLS), F32),
-            V((RZ, 2, 2, 2, KD, HALF), F32),
-            V((RZ, 2, 2, 4, KD, HALF), F32),
-            V((RZ, 2, 2, KD // 2, HALF), F32),
-            V((RZ, 2, 2, KD, HALF), F32),
-            V((RZ - 1, KD, COLS), F32),
+            V((RZ, 2, 2, 2, XR, HALF), F32),
+            V((RZ, 2, 2, 4, XR, HALF), F32),
+            V((RZ, 2, 2, 16, HALF), F32),
+            V((RZ, 2, 2, XR, HALF), F32),
+            V((RZ - 1, XR, COLS), F32),
+            V((4, 2, RY, RX, ZR, COLS), F32),
+            V((PLANE - 1, ZR, COLS), F32),
             V((KD, COLS), F32),
             V((128, 8, 128), F32),
             V((PLANE - 1, 8, 8, 128), F32),
@@ -401,6 +456,8 @@
             dma((RZ, 2, 8)),
             dma((8,)),
             dma((8,)),
+            dma((2, 16)),
+            dma((2, 16)),
             dma((4, 16)),
             dma((4, 16)),
         ],

time: 86.6 us -> 87.9 us (1.015)
  Pallas kernels: 81.6 us -> 82.8 us
    pallas_call x1, Pallas kernels: 81.6 us -> 82.8 us  [sketch_and_gram(): pl.pallas_call(kernel, out_shape=(jax.ShapeDtypeStruct((KD, COLS), F32),...]
where the time goes in v3:
time: 87.9 us; the launch traced here: 86.6 us
  Pallas kernels  82.8 us (94%)
  local copies, waits for them, and re-layouts  3.24 us (4%)
    pallas_call x1, Pallas kernels, sketch_and_gram(): pl.pallas_call(kernel, out_shape=(jax.ShapeDtypeStruct((KD, COLS), F32),...  82.8 us
    unnamed x2, local copies, waits for them, and re-layouts  3.24 us

profile of v3, /device:TPU:1, one launch (start us, length us, event | category | flops | bytes accessed | tf_op | source)
XLA Modules:
  0.0 86.6 jit_solution(12516576674801988706)
XLA Ops:
  0.6 82.8 %sketch_and_gram.1 = (f32[32,256]{1,0:T(8,128)}, f32[256,512]{1,0:T(8,128)}) custom-call(s32[8]{0:T(128)} %order_ref.1, bf16[512,8,128]{2,1,0:T(8,128)(2,1)} %bitcast.3, s32[2,8,128]{2,1,0:T(8,128)} %flip_ref.1, s32[32,128]{1,0:T(8,128)} %bitcast.4, s32[32,128]{1,0:T(8,128)} %bitcast.5), custom_call_target="tpu_custom_call" | custom-call | tf_op jit(solution)/shard_map/sketch_and_gram/pallas_call | solution.py:413
  83.4 1.4 %copy.9 = f32[32,256]{1,0:T(8,128)} copy(f32[32,256]{1,0:T(8,128)} %get-tuple-element.4) | data formatting | bytes 65536
  84.8 1.9 %copy.10 = f32[256,512]{1,0:T(8,128)} copy(f32[256,512]{1,0:T(8,128)} %get-tuple-element.5) | data formatting | bytes 1048576

commit v4 on v2

--- a/solution.py
+++ b/solution.py
@@ -28,7 +28,10 @@
 HALO = [(dx, dy) for dx in (-1, 0, 1) for dy in (-1, 0, 1) if (dx, dy) != (0, 0)]
 ORDER = (4, 3, 5, 2, 6, 1, 7, 0)
 CHUNKS = 4
-LAG_A2, LAG_B1, LAG_B2, LAG_B3 = 3, 5, 7, 9
+LAG_A2, LAG_B1, LAG_B2, LAG_B3 = 2, 4, 6, 8
+PAIRS = RZ // 2
+ZR = 8
+XR = KD - ZR
 BANDS = PLANES * STRATUM // 128
 
 
@@ -40,9 +43,9 @@
 
 def kernel(
     order_ref, vol_hbm, flip_ref, block_ref, offset_ref, sk_ref, gram_ref,
-    vol, halo, ext, codes, mover, zs, xs, tt_hi, tt_lo,
-    c, ra1, ra2, rb1, rb2, rz, other, gs, r1, p1, r2, p3, out,
-    ld_sem, h_send, h_recv, a_send, a_recv, z_send, z_recv, g_send, g_recv,
+    vol, halo, ext, tables, mover, zs, xs, tt_hi, tt_lo,
+    c, ra1, ra2, rb1, rb2, rz, rv, rw, other, gs, r1, p1, r2, p3, out,
+    ld_sem, h_send, h_recv, a_send, a_recv, z_send, z_recv, v_send, v_recv, g_send, g_recv,
 ):
     vx, vy, sj = lax.axis_index("vx"), lax.axis_index("vy"), lax.axis_index("subj")
     x, y = lax.rem(vx, RX), lax.div(vx, RX)
@@ -145,12 +148,31 @@
     lax.fori_loop(0, 8, own_planes, 0)
 
     code_t = (block_ref[...] * 16 + offset_ref[...]).astype(F32).T.astype(I32)
+    lane = lax.broadcasted_iota(I32, (1, 128), 1)
+    gx = vx * 2 + lane // EY - 1 + 32
+    gy = vy * 8 + lane % EY - 1 + 64
+    voxel = (((gx >> 1) & 15) * 8 + ((gy >> 3) & 7)) * 16 + (gx & 1) * 8 + (gy & 7)
+    off_lane = lane & 15
+    ej = lax.broadcasted_iota(I32, (128, PLANES * STRATUM), 0)
+    ek = lax.broadcasted_iota(I32, (128, PLANES * STRATUM), 1)
+    spread = jnp.where((ek >> 4) == ej, 1.0, 0.0).astype(BF16)
+    place = lax.broadcasted_iota(I32, (PLANE * KD, 128), 0) // KD
     for g in range(RZ):
-        for p in range(PLANE):
-            i = 2 * p + g // 4
-            codes[g, p * KD : (p + 1) * KD, :] = jnp.broadcast_to(
-                code_t[(g % 4) * KD : (g % 4 + 1) * KD, i : i + 1], (KD, 128)
-            )
+        code = jnp.concatenate(
+            [
+                jnp.broadcast_to(
+                    code_t[(g % 4) * KD : (g % 4 + 1) * KD, 2 * p + g // 4 : 2 * p + g // 4 + 1], (KD, 128)
+                )
+                for p in range(PLANE)
+            ],
+            axis=0,
+        )
+        sgn = parity_sign(((code & -16) + place) & voxel, (8, 4, 2, 1)).astype(BF16)
+        wide = jnp.dot(sgn, spread, preferred_element_type=F32)
+        pick = (code & 15) == off_lane
+        for k in range(BANDS):
+            at = slice(k * 128, (k + 1) * 128)
+            tables[g, :, at] = jnp.where(pick, wide[:, at], 0.0).astype(BF16)
 
     lanes = lax.broadcasted_iota(I32, (64, 512), 1)
     rows = lax.broadcasted_iota(I32, (64, 512), 0)
@@ -182,124 +204,150 @@
     lax.fori_loop(0, EY, x_planes, 0)
     lax.fori_loop(0, 2, y_planes, 0)
 
-    lane = lax.broadcasted_iota(I32, (1, 128), 1)
-    gx = vx * 2 + lane // EY - 1 + 32
-    gy = vy * 8 + lane % EY - 1 + 64
-    voxel = (((gx >> 1) & 15) * 8 + ((gy >> 3) & 7)) * 16 + (gx & 1) * 8 + (gy & 7)
-    off_lane = lane & 15
-    ej = lax.broadcasted_iota(I32, (128, PLANES * STRATUM), 0)
-    ek = lax.broadcasted_iota(I32, (128, PLANES * STRATUM), 1)
-    spread = jnp.where((ek >> 4) == ej, 1.0, 0.0).astype(BF16)
-    place = lax.broadcasted_iota(I32, (PLANE * KD, 128), 0) // KD
-
-    def group(o):
-        return lax.rem(vy + o, RZ)
-
-    def contribute(o):
-        g = group(o)
-        code = codes[g]
-        sgn = parity_sign(((code & -16) + place) & voxel, (8, 4, 2, 1)).astype(BF16)
-        wide = jnp.dot(sgn, spread, preferred_element_type=F32)
-        pick = (code & 15) == off_lane
-        s_mat = jnp.concatenate(
-            [jnp.where(pick, wide[:, k * 128 : (k + 1) * 128], 0.0).astype(BF16) for k in range(BANDS)], axis=1
-        )
-        r = jnp.dot(s_mat, tt_hi[g], preferred_element_type=F32)
-        r = r + jnp.dot(s_mat, tt_lo[g], preferred_element_type=F32)
-        c[g] = (r * (1.0 / 512.0)).reshape(RY, RX, KD, COLS)
+    def contribute(t):
+        g = lax.rem(vy + ORDER[t], RZ)
+        r = jnp.dot(tables[g], tt_hi[g], preferred_element_type=F32)
+        r = (r + jnp.dot(tables[g], tt_lo[g], preferred_element_type=F32)) * (1.0 / 512.0)
+        for p in range(PLANE):
+            dy, dx = lax.rem(p // RX - y + RY, RY), lax.rem(p % RX - x + RX, RX)
+            c[t, dy, dx] = r[p * KD : (p + 1) * KD]
 
     lanes_of = [pl.ds(0, HALF), pl.ds(HALF, HALF)]
-    x1, x2, x3 = lax.rem(x + 1, RX), lax.rem(x + 2, RX), lax.rem(x + 3, RX)
-    y1, y2, y3 = lax.rem(y + 1, RY), lax.rem(y + 2, RY), lax.rem(y + 3, RY)
-    A1, A2, B1, B2, ZC = {}, {}, {}, {}, {}
-
-    def sems(o, h, k):
-        return a_send.at[o, h, k], a_recv.at[o, h, k]
-
-    def start_a1(o):
-        g = group(o)
+    X, ZF = pl.ds(ZR, XR), pl.ds(0, ZR)
+    A1, A2, B1, B2, ZC, ZV, ZW = {}, {}, {}, {}, {}, {}, {}
+    WAYS = ((1, 1), (-1, 3))
+
+    def sems(u, h, k):
+        return a_send.at[u, h, k], a_recv.at[u, h, k]
+
+    def first(h, way):
+        return xy(way, 0) if h == 0 else xy(0, way)
+
+    def second(h, way):
+        return xy(0, way) if h == 0 else xy(way, 0)
+
+    def block(h, U, near_axis, other_axis):
+        return (U, other_axis, near_axis) if h == 0 else (U, near_axis, other_axis)
+
+    def start_a1(u):
+        U = pl.ds(2 * u, 2)
         for h in range(2):
-            L = lanes_of[h]
             for k in range(2):
-                cross = pl.ds(2 * k, 2)
-                if h == 0:
-                    src, dev = c.at[g, cross, x2, :, L], xy(1 - 2 * k, 0)
+                src = c.at[(*block(h, U, 2, pl.ds(2 * k, 2)), X, lanes_of[h])]
+                A1[u, h, k] = go(remote(src, ra1.at[u, h, k], *sems(u, h, k), first(h, WAYS[k][0])))
+
+    def do_a2(u):
+        U = pl.ds(2 * u, 2)
+        for h in range(2):
+            for k in range(2):
+                way, near_pos = WAYS[k]
+                A1[u, h, k].wait_recv()
+                at = (*block(h, U, near_pos, pl.ds(2 * k, 2)), X, lanes_of[h])
+                c[at] = c[at] + ra1[u, h, k]
+                src = c.at[(*block(h, U, near_pos, pl.ds(0, 4)), X, lanes_of[h])]
+                A2[u, h, k] = go(remote(src, ra2.at[u, h, k], *sems(u, h, 2 + k), first(h, way)))
+
+    def far(u, k):
+        rows = (16, XR - 16)[(k + u) % 2]
+        return pl.ds(ZR if k == 0 else ZR + XR - rows, rows), pl.ds(0, rows)
+
+    def do_b1(u):
+        U = pl.ds(2 * u, 2)
+        for h in range(2):
+            A2[u, h, 0].wait_recv()
+            A2[u, h, 1].wait_recv()
+            at = (*block(h, U, 0, pl.ds(0, 4)), X, lanes_of[h])
+            c[at] = c[at] + ra2[u, h, 0] + ra2[u, h, 1]
+            for k in range(2):
+                part, room = far(u, k)
+                src = c.at[(*block(h, U, 0, 2), part, lanes_of[h])]
+                B1[u, h, k] = go(remote(src, rb1.at[u, h, k, :, room], *sems(u, h, 4 + k), second(h, WAYS[k][0])))
+
+    def do_b2(u):
+        U = pl.ds(2 * u, 2)
+        for h in range(2):
+            for k in range(2):
+                way, near_pos = WAYS[k]
+                B1[u, h, k].wait_recv()
+                part, room = far(u, k)
+                at = (*block(h, U, 0, near_pos), part, lanes_of[h])
+                c[at] = c[at] + rb1[u, h, k, :, room]
+                src = c.at[(*block(h, U, 0, near_pos), X, lanes_of[h])]
+                B2[u, h, k] = go(remote(src, rb2.at[u, h, k], *sems(u, h, 6 + k), second(h, way)))
+
+    def do_b3(u):
+        U = pl.ds(2 * u, 2)
+        for h in range(2):
+            B2[u, h, 0].wait_recv()
+            B2[u, h, 1].wait_recv()
+            at = (U, 0, 0, X, lanes_of[h])
+            c[at] = c[at] + rb2[u, h, 0] + rb2[u, h, 1]
+        for t in (2 * u, 2 * u + 1):
+            o = ORDER[t]
+            if o:
+                ZC[o] = go(remote(c.at[t, 0, 0, X], rz.at[o - 1], z_send.at[o - 1], z_recv.at[o - 1], z_dev(o)))
+
+    def ring(n):
+        for b in range(2):
+            for k in range(2):
+                to = ORDER.index(5 - n if k == 0 else 3 + n)
+                if n == 1:
+                    own = pl.ds(2 * k + b, 1)
+                    src, dst = c.at[to, own, :, ZF], rv.at[0, b, k, pl.ds(0, 1)]
                 else:
-                    src, dev = c.at[g, y2, cross, :, L], xy(0, 1 - 2 * k)
-                A1[o, h, k] = go(remote(src, ra1.at[o, h, k], *sems(o, h, k), dev))
-
-    def do_a2(o):
-        g = group(o)
-        for h in range(2):
-            L = lanes_of[h]
-            for k in range(2):
-                A1[o, h, k].wait_recv()
-                cross = pl.ds(2 * k, 2)
-                if h == 0:
-                    nxt = (x1, x3)[k]
-                    c[g, cross, nxt, :, L] = c[g, cross, nxt, :, L] + ra1[o, h, k]
-                    src, dev = c.at[g, :, nxt, :, L], xy(1 - 2 * k, 0)
-                else:
-                    nxt = (y1, y3)[k]
-                    c[g, nxt, cross, :, L] = c[g, nxt, cross, :, L] + ra1[o, h, k]
-                    src, dev = c.at[g, nxt, :, :, L], xy(0, 1 - 2 * k)
-                A2[o, h, k] = go(remote(src, ra2.at[o, h, k], *sems(o, h, 2 + k), dev))
-
-    def do_b1(o):
-        g = group(o)
-        for h in range(2):
-            L = lanes_of[h]
-            A2[o, h, 0].wait_recv()
-            A2[o, h, 1].wait_recv()
-            if h == 0:
-                c[g, :, x, :, L] = c[g, :, x, :, L] + ra2[o, h, 0] + ra2[o, h, 1]
-            else:
-                c[g, y, :, :, L] = c[g, y, :, :, L] + ra2[o, h, 0] + ra2[o, h, 1]
-            for k in range(2):
-                part = pl.ds(16 * k, 16)
-                if h == 0:
-                    src, dev = c.at[g, y2, x, part, L], xy(0, 1 - 2 * k)
-                else:
-                    src, dev = c.at[g, y, x2, part, L], xy(1 - 2 * k, 0)
-                B1[o, h, k] = go(remote(src, rb1.at[o, h, k], *sems(o, h, 4 + k), dev))
-
-    def do_b2(o):
-        g = group(o)
-        for h in range(2):
-            L = lanes_of[h]
-            for k in range(2):
-                B1[o, h, k].wait_recv()
-                part = pl.ds(16 * k, 16)
-                if h == 0:
-                    nxt = (y1, y3)[k]
-                    c[g, nxt, x, part, L] = c[g, nxt, x, part, L] + rb1[o, h, k]
-                    src, dev = c.at[g, nxt, x, :, L], xy(0, 1 - 2 * k)
-                else:
-                    nxt = (x1, x3)[k]
-                    c[g, y, nxt, part, L] = c[g, y, nxt, part, L] + rb1[o, h, k]
-                    src, dev = c.at[g, y, nxt, :, L], xy(1 - 2 * k, 0)
-                B2[o, h, k] = go(remote(src, rb2.at[o, h, k], *sems(o, h, 6 + k), dev))
-
-    def do_b3(o):
-        g = group(o)
-        for h in range(2):
-            L = lanes_of[h]
-            B2[o, h, 0].wait_recv()
-            B2[o, h, 1].wait_recv()
-            c[g, y, x, :, L] = c[g, y, x, :, L] + rb2[o, h, 0] + rb2[o, h, 1]
-        if o:
-            ZC[o] = go(remote(c.at[g, y, x], rz.at[o - 1], z_send.at[o - 1], z_recv.at[o - 1], z_dev(o)))
-
-    stages = ((0, contribute), (0, start_a1), (LAG_A2, do_a2), (LAG_B1, do_b1), (LAG_B2, do_b2), (LAG_B3, do_b3))
-    for step in range(RZ + LAG_B3):
+                    at = b ^ k ^ 1 if n == 2 else b
+                    own = pl.ds(2 * at, 2)
+                    if n == 2 and b == 1:
+                        for i in range(2):
+                            ZV[1, i, k].wait_recv()
+                            c[to, 2 * k + i, :, ZF] = c[to, 2 * k + i, :, ZF] + rv[0, i, k, 0]
+                    elif n > 2:
+                        ZV[n - 1, b, k].wait_recv()
+                        c[to, own, :, ZF] = c[to, own, :, ZF] + rv[n - 2, b, k]
+                    src, dst = c.at[to, own, :, ZF], rv.at[n - 1, at, k]
+                piece = at if n == 2 else b
+                dev = z_dev(1 if k == 0 else RZ - 1)
+                i = 4 * (n - 1) + 2 * piece + k
+                ZV[n, piece, k] = go(remote(src, dst, v_send.at[0, i], v_recv.at[0, i], dev))
+
+    def spread_plane():
+        t = ORDER.index(0)
+        for b in range(2):
+            ZV[4, b, 0].wait_recv()
+            ZV[4, b, 1].wait_recv()
+            own = pl.ds(2 * b, 2)
+            c[t, own, :, ZF] = c[t, own, :, ZF] + rv[3, b, 0] + rv[3, b, 1]
+        for o in range(1, PLANE):
+            dy, dx = o // RX, o % RX
+            ZW[o] = go(remote(c.at[t, dy, dx, ZF], rw.at[o - 1], v_send.at[1, o], v_recv.at[1, o], xy(dx, dy)))
+
+    stages = ((LAG_A2, do_a2), (LAG_B1, do_b1), (LAG_B2, do_b2), (LAG_B3, do_b3))
+    ring_at = {1: 0, 2: 2, 3: 4, 4: 5}
+    for step in range(PAIRS + LAG_B3):
+        if step < PAIRS:
+            contribute(2 * step)
+            if step == 0:
+                ring(1)
+            contribute(2 * step + 1)
+            start_a1(step)
+        for n in (2, 3, 4):
+            if ring_at[n] == step:
+                ring(n)
         for lag, stage in stages:
-            if 0 <= step - lag < RZ:
-                stage(ORDER[step - lag])
-
-    total = c[vy, y, x]
+            if 0 <= step - lag < PAIRS:
+                stage(step - lag)
+        if step == 6:
+            spread_plane()
+
+    low = c[RZ - 1, 0, 0, ZF]
+    for o in range(1, PLANE):
+        ZW[o].wait_recv()
+        low = low + rw[o - 1]
+    high = c[RZ - 1, 0, 0, X]
     for o in ORDER[:-1]:
         ZC[o].wait_recv()
-        total = total + rz[o - 1]
+        high = high + rz[o - 1]
+    total = jnp.concatenate([low, high], axis=0)
     sk_ref[...] = total
 
     swap = go(remote(sk_ref, other, z_send.at[7], z_recv.at[7], partner))
@@ -375,18 +423,20 @@
             V((COLS * 2, 8, 128), BF16),
             V((8, 2, 8, 128), I32),
             V((EX, EY, 1, 128), F32),
-            V((RZ, PLANE * KD, 128), I32),
+            V((RZ, PLANE * KD, PLANES * STRATUM), BF16),
             V((512, 512), BF16),
             V((COLS * 16, 128), F32),
             V((EX, EY + 2, COLS, 128), F32),
             V((RZ, PLANES * STRATUM, COLS), BF16),
             V((RZ, PLANES * STRATUM, COLS), BF16),
             V((RZ, RY, RX, KD, COLS), F32),
-            V((RZ, 2, 2, 2, KD, HALF), F32),
-            V((RZ, 2, 2, 4, KD, HALF), F32),
-            V((RZ, 2, 2, KD // 2, HALF), F32),
-            V((RZ, 2, 2, KD, HALF), F32),
-            V((RZ - 1, KD, COLS), F32),
+            V((PAIRS, 2, 2, 2, 2, XR, HALF), F32),
+            V((PAIRS, 2, 2, 2, 4, XR, HALF), F32),
+            V((PAIRS, 2, 2, 2, 16, HALF), F32),
+            V((PAIRS, 2, 2, 2, XR, HALF), F32),
+            V((RZ - 1, XR, COLS), F32),
+            V((4, 2, 2, 2, RX, ZR, COLS), F32),
+            V((PLANE - 1, ZR, COLS), F32),
             V((KD, COLS), F32),
             V((128, 8, 128), F32),
             V((PLANE - 1, 8, 8, 128), F32),
@@ -397,10 +447,12 @@
             dma((CHUNKS,)),
             dma((8,)),
             dma((8,)),
-            dma((RZ, 2, 8)),
-            dma((RZ, 2, 8)),
+            dma((PAIRS, 2, 8)),
+            dma((PAIRS, 2, 8)),
             dma((8,)),
             dma((8,)),
+            dma((2, 16)),
+            dma((2, 16)),
             dma((4, 16)),
             dma((4, 16)),
         ],

time: 86.6 us -> 83.4 us (0.963)
  Pallas kernels: 81.6 us -> 79.2 us
    pallas_call x1, Pallas kernels: 81.6 us -> 79.2 us  [sketch_and_gram(): pl.pallas_call(kernel, out_shape=(jax.ShapeDtypeStruct((KD, COLS), F32),...]
where the time goes in v4:
time: 83.4 us; the launch traced here: 83.1 us
  Pallas kernels  79.2 us (95%)
  local copies, waits for them, and re-layouts  3.24 us (4%)
    pallas_call x1, Pallas kernels, sketch_and_gram(): pl.pallas_call(kernel, out_shape=(jax.ShapeDtypeStruct((KD, COLS), F32),...  79.2 us
    unnamed x2, local copies, waits for them, and re-layouts  3.24 us

profile of v4, /device:TPU:1, one launch (start us, length us, event | category | flops | bytes accessed | tf_op | source)
XLA Modules:
  0.0 83.1 jit_solution(15689851091782937299)
XLA Ops:
  0.6 79.2 %sketch_and_gram.1 = (f32[32,256]{1,0:T(8,128)}, f32[256,512]{1,0:T(8,128)}) custom-call(s32[8]{0:T(128)} %order_ref.1, bf16[512,8,128]{2,1,0:T(8,128)(2,1)} %bitcast.3, s32[2,8,128]{2,1,0:T(8,128)} %flip_ref.1, s32[32,128]{1,0:T(8,128)} %bitcast.4, s32[32,128]{1,0:T(8,128)} %bitcast.5), custom_call_target="tpu_custom_call" | custom-call | tf_op jit(solution)/shard_map/sketch_and_gram/pallas_call | solution.py:408
  79.9 1.4 %copy.9 = f32[32,256]{1,0:T(8,128)} copy(f32[32,256]{1,0:T(8,128)} %get-tuple-element.4) | data formatting | bytes 65536
  81.2 1.9 %copy.10 = f32[256,512]{1,0:T(8,128)} copy(f32[256,512]{1,0:T(8,128)} %get-tuple-element.5) | data formatting | bytes 1048576

commit v5 on v4

--- a/solution.py
+++ b/solution.py
@@ -30,6 +30,9 @@
 CHUNKS = 4
 LAG_A2, LAG_B1, LAG_B2, LAG_B3 = 2, 4, 6, 8
 PAIRS = RZ // 2
+PARTS = 4
+TILES = 8 // PARTS
+ROWS = COLS // PARTS
 ZR = 8
 XR = KD - ZR
 BANDS = PLANES * STRATUM // 128
@@ -44,7 +47,7 @@
 def kernel(
     order_ref, vol_hbm, flip_ref, block_ref, offset_ref, sk_ref, gram_ref,
     vol, halo, ext, tables, mover, zs, xs, tt_hi, tt_lo,
-    c, ra1, ra2, rb1, rb2, rz, rv, rw, other, gs, r1, p1, r2, p3, out,
+    c, ra1, ra2, rb1, rb2, rz, rv, rw, other, gs, r1, r2, p3, out,
     ld_sem, h_send, h_recv, a_send, a_recv, z_send, z_recv, v_send, v_recv, g_send, g_recv,
 ):
     vx, vy, sj = lax.axis_index("vx"), lax.axis_index("vy"), lax.axis_index("subj")
@@ -361,43 +364,50 @@
     mine = moved[:, :COLS] * first + moved[:, COLS:] * (1.0 - first)
     lhs = jnp.concatenate([mine[:KD], mine[:KD], mine[KD:]], axis=0).astype(BF16)
     rhs = jnp.concatenate([moved[:KD], moved[KD:], moved[:KD]], axis=0).astype(BF16)
-    part = lax.dot_general(lhs, rhs, (((0,), (0,)), ((), ())), preferred_element_type=F32)
-    for i in range(32):
-        for j in range(4):
-            gs[4 * i + j] = part[8 * i : 8 * i + 8, 128 * j : 128 * j + 128]
-
-    cp = []
-    for o in range(1, PLANE):
-        d = lax.rem(vx + o, PLANE)
-        cp.append(go(remote(gs.at[pl.ds(d * 8, 8)], r1.at[o - 1], g_send.at[0, o], g_recv.at[0, o], plane_dev(o))))
-    acc = gs[pl.ds(vx * 8, 8)]
-    for o in range(1, PLANE):
-        cp[o - 1].wait_recv()
-        acc = acc + r1[o - 1]
-    p1[...] = acc
-    cp = []
-    for o in range(1, RZ):
-        d = lax.rem(vy + o, RZ)
-        cp.append(go(remote(p1.at[d], r2.at[o - 1], g_send.at[1, o], g_recv.at[1, o], z_dev(o))))
-    acc = p1[vy]
-    for o in range(1, RZ):
-        cp[o - 1].wait_recv()
-        acc = acc + r2[o - 1]
-    p3[vy] = acc * (1.0 / 4096.0)
-    cp = []
-    for o in range(1, RZ):
-        cp.append(go(remote(p3.at[vy], p3.at[vy], g_send.at[2, o], g_recv.at[2, o], z_dev(o))))
-    for o in range(1, RZ):
-        cp[o - 1].wait_recv()
-    cp = []
-    for o in range(1, PLANE):
-        cp.append(go(remote(p3, out.at[pl.ds(vx * 8, 8)], g_send.at[3, o], g_recv.at[3, o], plane_dev(o))))
-    out[pl.ds(vx * 8, 8)] = p3[...]
-    for o in range(1, PLANE):
-        cp[o - 1].wait_recv()
-    for i in range(32):
-        for j in range(4):
-            gram_ref[8 * i : 8 * i + 8, 128 * j : 128 * j + 128] = out[4 * i + j]
+    around = [(dy, dx) for dy in range(RY) for dx in range(RX) if dy or dx]
+    around.sort(key=lambda d: -min(d[0], RY - d[0]) - min(d[1], RX - d[1]))
+    owner = [lax.rem(y + dy, RY) * RX + lax.rem(x + dx, RX) for dy, dx in around]
+    far_z = (4, 3, 5, 2, 6, 1, 7)
+    G1, G2, G3 = {}, {}, {}
+
+    def gsems(n, q, i):
+        return g_send.at[n, q, i], g_recv.at[n, q, i]
+
+    for q in range(PARTS):
+        part = lax.dot_general(
+            lhs[:, q * ROWS : (q + 1) * ROWS], rhs, (((0,), (0,)), ((), ())), preferred_element_type=F32
+        )
+        for i in range(ROWS // 8):
+            for j in range(4):
+                gs[q, 4 * i + j] = part[8 * i : 8 * i + 8, 128 * j : 128 * j + 128]
+        for i, (dy, dx) in enumerate(around):
+            src = gs.at[q, pl.ds(owner[i] * TILES, TILES)]
+            G1[q, i] = go(remote(src, r1.at[q, i], *gsems(0, q, i), xy(dx, dy)))
+    for q in range(PARTS):
+        acc = gs[q, pl.ds(vx * TILES, TILES)]
+        for i in range(PLANE - 1):
+            G1[q, i].wait_recv()
+            acc = acc + r1[q, i]
+        r2[q, vy] = acc
+        for i, o in enumerate(far_z):
+            G2[q, i] = go(remote(r2.at[q, vy], r2.at[q, vy], *gsems(1, q, i), z_dev(o)))
+    for q in range(PARTS):
+        for i in range(RZ - 1):
+            G2[q, i].wait_recv()
+        acc = r2[q, 0]
+        for i in range(1, RZ):
+            acc = acc + r2[q, i]
+        mine_at = pl.ds(vx * TILES, TILES)
+        p3[q] = acc * (1.0 / 4096.0)
+        for i, (dy, dx) in enumerate(around):
+            G3[q, i] = go(remote(p3.at[q], out.at[q, mine_at], *gsems(2, q, i), xy(dx, dy)))
+        out[q, mine_at] = p3[q]
+    for q in range(PARTS):
+        for i in range(PLANE - 1):
+            G3[q, i].wait_recv()
+        for i in range(ROWS // 8):
+            for j in range(4):
+                gram_ref[q * ROWS + 8 * i : q * ROWS + 8 * i + 8, 128 * j : 128 * j + 128] = out[q, 4 * i + j]
     for copy in started:
         copy.wait_send()
 
@@ -438,12 +448,11 @@
             V((4, 2, 2, 2, RX, ZR, COLS), F32),
             V((PLANE - 1, ZR, COLS), F32),
             V((KD, COLS), F32),
-            V((128, 8, 128), F32),
-            V((PLANE - 1, 8, 8, 128), F32),
-            V((8, 8, 128), F32),
-            V((RZ - 1, 8, 128), F32),
-            V((8, 8, 128), F32),
-            V((128, 8, 128), F32),
+            V((PARTS, PLANE * TILES, 8, 128), F32),
+            V((PARTS, PLANE - 1, TILES, 8, 128), F32),
+            V((PARTS, RZ, TILES, 8, 128), F32),
+            V((PARTS, TILES, 8, 128), F32),
+            V((PARTS, PLANE * TILES, 8, 128), F32),
             dma((CHUNKS,)),
             dma((8,)),
             dma((8,)),
@@ -453,8 +462,8 @@
             dma((8,)),
             dma((2, 16)),
             dma((2, 16)),
-            dma((4, 16)),
-            dma((4, 16)),
+            dma((3, PARTS, 16)),
+            dma((3, PARTS, 16)),
         ],
         compiler_params=pltpu.CompilerParams(
             collective_id=0, has_side_effects=True, vmem_limit_bytes=60 * 1024 * 1024

time: 83.4 us -> 79.8 us (0.957)
  Pallas kernels: 79.2 us -> 75.6 us
    pallas_call x1, Pallas kernels: 79.2 us -> 75.6 us  [sketch_and_gram(): pl.pallas_call(kernel, out_shape=(jax.ShapeDtypeStruct((KD, COLS), F32),...]
where the time goes in v5:
time: 79.8 us; the launch traced here: 79.5 us
  Pallas kernels  75.6 us (95%)
  local copies, waits for them, and re-layouts  3.24 us (4%)
    pallas_call x1, Pallas kernels, sketch_and_gram(): pl.pallas_call(kernel, out_shape=(jax.ShapeDtypeStruct((KD, COLS), F32),...  75.6 us
    unnamed x2, local copies, waits for them, and re-layouts  3.24 us

profile of v5, /device:TPU:1, one launch (start us, length us, event | category | flops | bytes accessed | tf_op | source)
XLA Modules:
  0.0 79.5 jit_solution(13383590443792669955)
XLA Ops:
  0.6 75.6 %sketch_and_gram.1 = (f32[32,256]{1,0:T(8,128)}, f32[256,512]{1,0:T(8,128)}) custom-call(s32[8]{0:T(128)} %order_ref.1, bf16[512,8,128]{2,1,0:T(8,128)(2,1)} %bitcast.3, s32[2,8,128]{2,1,0:T(8,128)} %flip_ref.1, s32[32,128]{1,0:T(8,128)} %bitcast.4, s32[32,128]{1,0:T(8,128)} %bitcast.5), custom_call_target="tpu_custom_call" | custom-call | tf_op jit(solution)/shard_map/sketch_and_gram/pallas_call | solution.py:418
  76.2 1.4 %copy.9 = f32[32,256]{1,0:T(8,128)} copy(f32[32,256]{1,0:T(8,128)} %get-tuple-element.4) | data formatting | bytes 65536
  77.6 1.9 %copy.10 = f32[256,512]{1,0:T(8,128)} copy(f32[256,512]{1,0:T(8,128)} %get-tuple-element.5) | data formatting | bytes 1048576

commit v6 on v5

--- a/solution.py
+++ b/solution.py
@@ -45,10 +45,10 @@
 
 
 def kernel(
-    order_ref, vol_hbm, flip_ref, block_ref, offset_ref, sk_ref, gram_ref,
-    vol, halo, ext, tables, mover, zs, xs, tt_hi, tt_lo,
+    order_hbm, vol_hbm, flip_hbm, block_hbm, offset_hbm, sk_ref, gram_ref,
+    order_ref, flip_ref, block_ref, offset_ref, vol, halo, ext, tables, mover, zs, xs, tt_hi, tt_lo,
     c, ra1, ra2, rb1, rb2, rz, rv, rw, other, gs, r1, r2, p3, out,
-    ld_sem, h_send, h_recv, a_send, a_recv, z_send, z_recv, v_send, v_recv, g_send, g_recv,
+    ld_sem, sends, a_recv, v_recv, g_recv, recvs,
 ):
     vx, vy, sj = lax.axis_index("vx"), lax.axis_index("vy"), lax.axis_index("subj")
     x, y = lax.rem(vx, RX), lax.div(vx, RX)
@@ -67,12 +67,21 @@
 
     partner = (vx, vy, 1 - sj)
 
+    small = [
+        pltpu.make_async_copy(src, dst, ld_sem.at[CHUNKS + i])
+        for i, (src, dst) in enumerate(
+            ((flip_hbm, flip_ref), (block_hbm, block_ref), (offset_hbm, offset_ref), (order_hbm, order_ref))
+        )
+    ]
+    small[0].start()
     loads = []
     per = COLS * 2 // CHUNKS
     for i in range(CHUNKS):
         part = pl.ds(i * per, per)
         loads.append(pltpu.make_async_copy(vol_hbm.at[part], vol.at[part], ld_sem.at[i]))
         loads[-1].start()
+    for copy in small[1:]:
+        copy.start()
 
     barrier = pltpu.get_barrier_semaphore()
     peers = [plane_dev(o) for o in range(1, PLANE)] + [z_dev(o) for o in range(1, RZ)] + [partner]
@@ -80,6 +89,7 @@
     for d in peers:
         pl.semaphore_signal(barrier, inc=1, device_id=d, device_id_type=MESH)
 
+    small[0].wait()
     for bx in range(2):
         for by in range(8):
             ext[bx + 1, by + 1] = (2 * flip_ref[bx, pl.ds(by, 1), :] - 1).astype(F32)
@@ -107,18 +117,18 @@
             src_ref=src, dst_ref=dst, send_sem=ssem, recv_sem=rsem, device_id=dev, device_id_type=MESH
         )
 
-    started = []
-
-    def go(copy):
-        copy.start()
-        started.append(copy)
-        return copy
+    def go(src, dst, kind, rsem, dev):
+        remote(src, dst, sends.at[kind], rsem, dev).start()
+
+    def arrive(whole, rsem):
+        remote(whole, whole, sends.at[0], rsem, partner).wait_recv()
+
+    def sent(whole, kind):
+        remote(whole, whole, sends.at[kind], recvs.at[0], partner).wait_send()
 
     pl.semaphore_wait(barrier, len(peers))
-    signs = [
-        go(remote(flip_ref, halo.at[i], h_send.at[i], h_recv.at[i], near(dx, dy)))
-        for i, (dx, dy) in enumerate(HALO)
-    ]
+    for i, (dx, dy) in enumerate(HALO):
+        go(flip_ref, halo.at[i], 0, recvs.at[0], near(dx, dy))
 
     zero = jnp.zeros((COLS, 128), F32)
     for ex in range(EX):
@@ -150,6 +160,8 @@
 
     lax.fori_loop(0, 8, own_planes, 0)
 
+    for copy in small[1:]:
+        copy.wait()
     code_t = (block_ref[...] * 16 + offset_ref[...]).astype(F32).T.astype(I32)
     lane = lax.broadcasted_iota(I32, (1, 128), 1)
     gx = vx * 2 + lane // EY - 1 + 32
@@ -184,8 +196,7 @@
 
     okx = {-1: jnp.where(vx > 0, 1, 0), 0: 1, 1: jnp.where(vx < PLANE - 1, 1, 0)}
     oky = {-1: jnp.where(vy > 0, 1, 0), 0: 1, 1: jnp.where(vy < RZ - 1, 1, 0)}
-    for copy in signs:
-        copy.wait_recv()
+    arrive(halo, recvs.at[0])
     for i, (dx, dy) in enumerate(HALO):
         ok = (okx[-dx] * oky[-dy]).astype(F32)
         xpos = {-1: [(0, 1)], 0: [(1, 0), (2, 1)], 1: [(3, 0)]}[-dx]
@@ -217,11 +228,7 @@
 
     lanes_of = [pl.ds(0, HALF), pl.ds(HALF, HALF)]
     X, ZF = pl.ds(ZR, XR), pl.ds(0, ZR)
-    A1, A2, B1, B2, ZC, ZV, ZW = {}, {}, {}, {}, {}, {}, {}
     WAYS = ((1, 1), (-1, 3))
-
-    def sems(u, h, k):
-        return a_send.at[u, h, k], a_recv.at[u, h, k]
 
     def first(h, way):
         return xy(way, 0) if h == 0 else xy(0, way)
@@ -237,18 +244,18 @@
         for h in range(2):
             for k in range(2):
                 src = c.at[(*block(h, U, 2, pl.ds(2 * k, 2)), X, lanes_of[h])]
-                A1[u, h, k] = go(remote(src, ra1.at[u, h, k], *sems(u, h, k), first(h, WAYS[k][0])))
+                go(src, ra1.at[u, h, k], 1, a_recv.at[0, u], first(h, WAYS[k][0]))
 
     def do_a2(u):
         U = pl.ds(2 * u, 2)
+        arrive(ra1.at[u], a_recv.at[0, u])
         for h in range(2):
             for k in range(2):
                 way, near_pos = WAYS[k]
-                A1[u, h, k].wait_recv()
                 at = (*block(h, U, near_pos, pl.ds(2 * k, 2)), X, lanes_of[h])
                 c[at] = c[at] + ra1[u, h, k]
                 src = c.at[(*block(h, U, near_pos, pl.ds(0, 4)), X, lanes_of[h])]
-                A2[u, h, k] = go(remote(src, ra2.at[u, h, k], *sems(u, h, 2 + k), first(h, way)))
+                go(src, ra2.at[u, h, k], 2, a_recv.at[1, u], first(h, way))
 
     def far(u, k):
         rows = (16, XR - 16)[(k + u) % 2]
@@ -256,39 +263,37 @@
 
     def do_b1(u):
         U = pl.ds(2 * u, 2)
+        arrive(ra2.at[u], a_recv.at[1, u])
         for h in range(2):
-            A2[u, h, 0].wait_recv()
-            A2[u, h, 1].wait_recv()
             at = (*block(h, U, 0, pl.ds(0, 4)), X, lanes_of[h])
             c[at] = c[at] + ra2[u, h, 0] + ra2[u, h, 1]
             for k in range(2):
                 part, room = far(u, k)
                 src = c.at[(*block(h, U, 0, 2), part, lanes_of[h])]
-                B1[u, h, k] = go(remote(src, rb1.at[u, h, k, :, room], *sems(u, h, 4 + k), second(h, WAYS[k][0])))
+                go(src, rb1.at[u, h, k, :, room], 3, a_recv.at[2, u], second(h, WAYS[k][0]))
 
     def do_b2(u):
         U = pl.ds(2 * u, 2)
+        arrive(rb2.at[u, :, 0], a_recv.at[2, u])
         for h in range(2):
             for k in range(2):
                 way, near_pos = WAYS[k]
-                B1[u, h, k].wait_recv()
                 part, room = far(u, k)
                 at = (*block(h, U, 0, near_pos), part, lanes_of[h])
                 c[at] = c[at] + rb1[u, h, k, :, room]
                 src = c.at[(*block(h, U, 0, near_pos), X, lanes_of[h])]
-                B2[u, h, k] = go(remote(src, rb2.at[u, h, k], *sems(u, h, 6 + k), second(h, way)))
+                go(src, rb2.at[u, h, k], 4, a_recv.at[3, u], second(h, way))
 
     def do_b3(u):
         U = pl.ds(2 * u, 2)
+        arrive(rb2.at[u], a_recv.at[3, u])
         for h in range(2):
-            B2[u, h, 0].wait_recv()
-            B2[u, h, 1].wait_recv()
             at = (U, 0, 0, X, lanes_of[h])
             c[at] = c[at] + rb2[u, h, 0] + rb2[u, h, 1]
         for t in (2 * u, 2 * u + 1):
             o = ORDER[t]
             if o:
-                ZC[o] = go(remote(c.at[t, 0, 0, X], rz.at[o - 1], z_send.at[o - 1], z_recv.at[o - 1], z_dev(o)))
+                go(c.at[t, 0, 0, X], rz.at[o - 1], 5, recvs.at[1], z_dev(o))
 
     def ring(n):
         for b in range(2):
@@ -301,28 +306,27 @@
                     at = b ^ k ^ 1 if n == 2 else b
                     own = pl.ds(2 * at, 2)
                     if n == 2 and b == 1:
+                        arrive(rv.at[0, :, k, 0], v_recv.at[0, 0, k])
                         for i in range(2):
-                            ZV[1, i, k].wait_recv()
                             c[to, 2 * k + i, :, ZF] = c[to, 2 * k + i, :, ZF] + rv[0, i, k, 0]
                     elif n > 2:
-                        ZV[n - 1, b, k].wait_recv()
+                        arrive(rv.at[n - 2, b, k], v_recv.at[n - 2, b, k])
                         c[to, own, :, ZF] = c[to, own, :, ZF] + rv[n - 2, b, k]
                     src, dst = c.at[to, own, :, ZF], rv.at[n - 1, at, k]
                 piece = at if n == 2 else b
                 dev = z_dev(1 if k == 0 else RZ - 1)
-                i = 4 * (n - 1) + 2 * piece + k
-                ZV[n, piece, k] = go(remote(src, dst, v_send.at[0, i], v_recv.at[0, i], dev))
+                go(src, dst, 6 if n == 1 else 7, v_recv.at[n - 1, 0 if n == 1 else piece, k], dev)
 
     def spread_plane():
         t = ORDER.index(0)
         for b in range(2):
-            ZV[4, b, 0].wait_recv()
-            ZV[4, b, 1].wait_recv()
+            arrive(rv.at[3, b, 0], v_recv.at[3, b, 0])
+            arrive(rv.at[3, b, 1], v_recv.at[3, b, 1])
             own = pl.ds(2 * b, 2)
             c[t, own, :, ZF] = c[t, own, :, ZF] + rv[3, b, 0] + rv[3, b, 1]
         for o in range(1, PLANE):
             dy, dx = o // RX, o % RX
-            ZW[o] = go(remote(c.at[t, dy, dx, ZF], rw.at[o - 1], v_send.at[1, o], v_recv.at[1, o], xy(dx, dy)))
+            go(c.at[t, dy, dx, ZF], rw.at[o - 1], 8, recvs.at[2], xy(dx, dy))
 
     stages = ((LAG_A2, do_a2), (LAG_B1, do_b1), (LAG_B2, do_b2), (LAG_B3, do_b3))
     ring_at = {1: 0, 2: 2, 3: 4, 4: 5}
@@ -343,18 +347,18 @@
             spread_plane()
 
     low = c[RZ - 1, 0, 0, ZF]
+    arrive(rw, recvs.at[2])
     for o in range(1, PLANE):
-        ZW[o].wait_recv()
         low = low + rw[o - 1]
     high = c[RZ - 1, 0, 0, X]
+    arrive(rz, recvs.at[1])
     for o in ORDER[:-1]:
-        ZC[o].wait_recv()
         high = high + rz[o - 1]
     total = jnp.concatenate([low, high], axis=0)
     sk_ref[...] = total
 
-    swap = go(remote(sk_ref, other, z_send.at[7], z_recv.at[7], partner))
-    swap.wait_recv()
+    go(sk_ref, other, 9, recvs.at[3], partner)
+    arrive(other, recvs.at[3])
     theirs = other[...]
     first = jnp.where(sj == 0, 1.0, 0.0)
     left = total * first + theirs * (1.0 - first)
@@ -368,10 +372,6 @@
     around.sort(key=lambda d: -min(d[0], RY - d[0]) - min(d[1], RX - d[1]))
     owner = [lax.rem(y + dy, RY) * RX + lax.rem(x + dx, RX) for dy, dx in around]
     far_z = (4, 3, 5, 2, 6, 1, 7)
-    G1, G2, G3 = {}, {}, {}
-
-    def gsems(n, q, i):
-        return g_send.at[n, q, i], g_recv.at[n, q, i]
 
     for q in range(PARTS):
         part = lax.dot_general(
@@ -382,34 +382,33 @@
                 gs[q, 4 * i + j] = part[8 * i : 8 * i + 8, 128 * j : 128 * j + 128]
         for i, (dy, dx) in enumerate(around):
             src = gs.at[q, pl.ds(owner[i] * TILES, TILES)]
-            G1[q, i] = go(remote(src, r1.at[q, i], *gsems(0, q, i), xy(dx, dy)))
+            go(src, r1.at[q, i], 10, g_recv.at[0, q], xy(dx, dy))
     for q in range(PARTS):
         acc = gs[q, pl.ds(vx * TILES, TILES)]
+        arrive(r1.at[q], g_recv.at[0, q])
         for i in range(PLANE - 1):
-            G1[q, i].wait_recv()
             acc = acc + r1[q, i]
         r2[q, vy] = acc
-        for i, o in enumerate(far_z):
-            G2[q, i] = go(remote(r2.at[q, vy], r2.at[q, vy], *gsems(1, q, i), z_dev(o)))
+        for o in far_z:
+            go(r2.at[q, vy], r2.at[q, vy], 11, g_recv.at[1, q], z_dev(o))
     for q in range(PARTS):
-        for i in range(RZ - 1):
-            G2[q, i].wait_recv()
+        arrive(r2.at[q, pl.ds(0, RZ - 1)], g_recv.at[1, q])
         acc = r2[q, 0]
         for i in range(1, RZ):
             acc = acc + r2[q, i]
         mine_at = pl.ds(vx * TILES, TILES)
         p3[q] = acc * (1.0 / 4096.0)
-        for i, (dy, dx) in enumerate(around):
-            G3[q, i] = go(remote(p3.at[q], out.at[q, mine_at], *gsems(2, q, i), xy(dx, dy)))
+        for dy, dx in around:
+            go(p3.at[q], out.at[q, mine_at], 12, g_recv.at[2, q], xy(dx, dy))
         out[q, mine_at] = p3[q]
     for q in range(PARTS):
-        for i in range(PLANE - 1):
-            G3[q, i].wait_recv()
+        arrive(r1.at[q], g_recv.at[2, q])
         for i in range(ROWS // 8):
             for j in range(4):
                 gram_ref[q * ROWS + 8 * i : q * ROWS + 8 * i + 8, 128 * j : 128 * j + 128] = out[q, 4 * i + j]
-    for copy in started:
-        copy.wait_send()
+    whole = (halo, ra1, ra2, rb2.at[:, :, 0], rb2, rz, rv.at[0, :, :, 0], rv.at[pl.ds(1, 3)], rw, other, r1)
+    for kind, ref in enumerate((*whole, r2.at[:, pl.ds(0, RZ - 1)], r1)):
+        sent(ref, kind)
 
 
 def sketch_and_gram(order, vol, flip, block, offset):
@@ -421,15 +420,13 @@
             jax.ShapeDtypeStruct((KD, COLS), F32),
             jax.ShapeDtypeStruct((COLS, 2 * COLS), F32),
         ),
-        in_specs=[
-            pl.BlockSpec(memory_space=pltpu.SMEM),
-            pl.BlockSpec(memory_space=pl.ANY),
-            pl.BlockSpec(memory_space=V),
-            pl.BlockSpec(memory_space=V),
-            pl.BlockSpec(memory_space=V),
-        ],
+        in_specs=[pl.BlockSpec(memory_space=pl.ANY)] * 5,
         out_specs=(pl.BlockSpec(memory_space=V), pl.BlockSpec(memory_space=V)),
         scratch_shapes=[
+            pltpu.SMEM((8,), I32),
+            V((2, 8, 128), I32),
+            V((32, 128), I32),
+            V((32, 128), I32),
             V((COLS * 2, 8, 128), BF16),
             V((8, 2, 8, 128), I32),
             V((EX, EY, 1, 128), F32),
@@ -453,17 +450,12 @@
             V((PARTS, RZ, TILES, 8, 128), F32),
             V((PARTS, TILES, 8, 128), F32),
             V((PARTS, PLANE * TILES, 8, 128), F32),
-            dma((CHUNKS,)),
-            dma((8,)),
-            dma((8,)),
-            dma((PAIRS, 2, 8)),
-            dma((PAIRS, 2, 8)),
-            dma((8,)),
-            dma((8,)),
-            dma((2, 16)),
-            dma((2, 16)),
-            dma((3, PARTS, 16)),
-            dma((3, PARTS, 16)),
+            dma((CHUNKS + 4,)),
+            dma((13,)),
+            dma((4, PAIRS)),
+            dma((4, 2, 2)),
+            dma((3, PARTS)),
+            dma((4,)),
         ],
         compiler_params=pltpu.CompilerParams(
             collective_id=0, has_side_effects=True, vmem_limit_bytes=60 * 1024 * 1024

time: 79.8 us -> 74 us (0.927)
  Pallas kernels: 75.6 us -> 69.9 us
    pallas_call x1, Pallas kernels: 75.6 us -> 69.9 us  [sketch_and_gram(): pl.pallas_call(kernel, out_shape=(jax.ShapeDtypeStruct((KD, COLS), F32),...]
where the time goes in v6:
time: 74 us; the launch traced here: 73.7 us
  Pallas kernels  69.9 us (94%)
  local copies, waits for them, and re-layouts  3.24 us (4%)
    pallas_call x1, Pallas kernels, sketch_and_gram(): pl.pallas_call(kernel, out_shape=(jax.ShapeDtypeStruct((KD, COLS), F32),...  69.9 us
    unnamed x2, local copies, waits for them, and re-layouts  3.24 us

profile of v6, /device:TPU:1, one launch (start us, length us, event | category | flops | bytes accessed | tf_op | source)
XLA Modules:
  0.0 73.7 jit_solution(15917149934404684851)
XLA Ops:
  0.6 69.9 %sketch_and_gram.1 = (f32[32,256]{1,0:T(8,128)}, f32[256,512]{1,0:T(8,128)}) custom-call(s32[8]{0:T(128)} %order_hbm.1, bf16[512,8,128]{2,1,0:T(8,128)(2,1)} %bitcast.3, s32[2,8,128]{2,1,0:T(8,128)} %flip_hbm.1, s32[32,128]{1,0:T(8,128)} %bitcast.4, s32[32,128]{1,0:T(8,128)} %bitcast.5), custom_call_target="tpu_custom_call" | custom-call | tf_op jit(solution)/shard_map/sketch_and_gram/pallas_call | solution.py:417
  70.5 1.4 %copy.9 = f32[32,256]{1,0:T(8,128)} copy(f32[32,256]{1,0:T(8,128)} %get-tuple-element.4) | data formatting | bytes 65536
  71.9 1.9 %copy.10 = f32[256,512]{1,0:T(8,128)} copy(f32[256,512]{1,0:T(8,128)} %get-tuple-element.5) | data formatting | bytes 1048576

commit v7 on v6

--- a/solution.py
+++ b/solution.py
@@ -47,7 +47,7 @@
 def kernel(
     order_hbm, vol_hbm, flip_hbm, block_hbm, offset_hbm, sk_ref, gram_ref,
     order_ref, flip_ref, block_ref, offset_ref, vol, halo, ext, tables, mover, zs, xs, tt_hi, tt_lo,
-    c, ra1, ra2, rb1, rb2, rz, rv, rw, other, gs, r1, r2, p3, out,
+    c, ra1, ra2, rb1, rb2, rz, rv, rw, packed, other, gs, r1, r2, p3, out,
     ld_sem, sends, a_recv, v_recv, g_recv, recvs,
 ):
     vx, vy, sj = lax.axis_index("vx"), lax.axis_index("vy"), lax.axis_index("subj")
@@ -329,7 +329,7 @@
             go(c.at[t, dy, dx, ZF], rw.at[o - 1], 8, recvs.at[2], xy(dx, dy))
 
     stages = ((LAG_A2, do_a2), (LAG_B1, do_b1), (LAG_B2, do_b2), (LAG_B3, do_b3))
-    ring_at = {1: 0, 2: 2, 3: 4, 4: 5}
+    ring_at = {1: 0, 2: 2, 3: 4, 4: 6}
     for step in range(PAIRS + LAG_B3):
         if step < PAIRS:
             contribute(2 * step)
@@ -343,7 +343,7 @@
         for lag, stage in stages:
             if 0 <= step - lag < PAIRS:
                 stage(step - lag)
-        if step == 6:
+        if step == 8:
             spread_plane()
 
     low = c[RZ - 1, 0, 0, ZF]
@@ -357,15 +357,15 @@
     total = jnp.concatenate([low, high], axis=0)
     sk_ref[...] = total
 
-    go(sk_ref, other, 9, recvs.at[3], partner)
+    mine_hi, mine_lo = split2(total)
+    packed[:KD], packed[KD:] = mine_hi, mine_lo
+    go(packed, other, 9, recvs.at[3], partner)
+    left = jnp.where(sj == 0, 1.0, 0.0)
+    own_half = jnp.concatenate([mine_hi, mine_lo], axis=0)
+    moved = jnp.dot(own_half, mover[pl.ds(sj * COLS, COLS)], preferred_element_type=F32)
     arrive(other, recvs.at[3])
-    theirs = other[...]
-    first = jnp.where(sj == 0, 1.0, 0.0)
-    left = total * first + theirs * (1.0 - first)
-    right = theirs * first + total * (1.0 - first)
-    parts = jnp.concatenate(split2(jnp.concatenate([left, right], axis=1)), axis=0)
-    moved = jnp.dot(parts, mover[...], preferred_element_type=F32)
-    mine = moved[:, :COLS] * first + moved[:, COLS:] * (1.0 - first)
+    moved = moved + jnp.dot(other[...], mover[pl.ds((1 - sj) * COLS, COLS)], preferred_element_type=F32)
+    mine = moved[:, :COLS] * left + moved[:, COLS:] * (1.0 - left)
     lhs = jnp.concatenate([mine[:KD], mine[:KD], mine[KD:]], axis=0).astype(BF16)
     rhs = jnp.concatenate([moved[:KD], moved[KD:], moved[:KD]], axis=0).astype(BF16)
     around = [(dy, dx) for dy in range(RY) for dx in range(RX) if dy or dx]
@@ -444,7 +444,8 @@
             V((RZ - 1, XR, COLS), F32),
             V((4, 2, 2, 2, RX, ZR, COLS), F32),
             V((PLANE - 1, ZR, COLS), F32),
-            V((KD, COLS), F32),
+            V((2 * KD, COLS), BF16),
+            V((2 * KD, COLS), BF16),
             V((PARTS, PLANE * TILES, 8, 128), F32),
             V((PARTS, PLANE - 1, TILES, 8, 128), F32),
             V((PARTS, RZ, TILES, 8, 128), F32),
@@ -464,14 +465,34 @@
     )(order, vol, flip, block, offset)
 
 
+def write_kernel(sk, gram, sk_out, gram_out, sem):
+    copies = [pltpu.make_async_copy(gram, gram_out, sem.at[0]), pltpu.make_async_copy(sk, sk_out, sem.at[1])]
+    for copy in copies:
+        copy.start()
+    for copy in copies:
+        copy.wait()
+
+
+def write_out(sk, gram):
+    return pl.pallas_call(
+        write_kernel,
+        out_shape=(jax.ShapeDtypeStruct(sk.shape, sk.dtype), jax.ShapeDtypeStruct(gram.shape, gram.dtype)),
+        in_specs=[pl.BlockSpec(memory_space=pltpu.VMEM)] * 2,
+        out_specs=(pl.BlockSpec(memory_space=pl.ANY), pl.BlockSpec(memory_space=pl.ANY)),
+        scratch_shapes=[pltpu.SemaphoreType.DMA((2,))],
+        name="write_out",
+    )(sk, gram)
+
+
 def on_device(volumes, flip_bits, hadamard_block, stratum_offset, subject_order):
-    return sketch_and_gram(
+    sk, gram = sketch_and_gram(
         subject_order,
         volumes.reshape(COLS * 2, 8, 128),
         flip_bits,
         hadamard_block.reshape(32, 128),
         stratum_offset.reshape(32, 128),
     )
+    return write_out(sk, gram)
 
 
 def solution(mesh):

time: 74 us -> 71.5 us (0.966)
  local copies, waits for them, and re-layouts: 3.24 us -> 0 us
  Pallas kernels: 69.9 us -> 70.7 us
    unnamed x2 -> x0, local copies, waits for them, and re-layouts: 3.24 us -> none
    pallas_call x0 -> x1, Pallas kernels: none -> 1.87 us  [write_out(): pl.pallas_call(write_kernel, out_shape=(jax.ShapeDtypeStruct(sk.shape, sk...]
    pallas_call x1, Pallas kernels: 69.9 us -> 68.8 us  [sketch_and_gram(): pl.pallas_call(kernel, out_shape=(jax.ShapeDtypeStruct((KD, COLS), F32),...]
where the time goes in v7:
time: 71.5 us; the launch traced here: 71.3 us
  Pallas kernels  70.7 us (99%)
    pallas_call x1, Pallas kernels, sketch_and_gram(): pl.pallas_call(kernel, out_shape=(jax.ShapeDtypeStruct((KD, COLS), F32),...  68.8 us
    pallas_call x1, Pallas kernels, write_out(): pl.pallas_call(write_kernel, out_shape=(jax.ShapeDtypeStruct(sk.shape, sk...  1.87 us

profile of v7, /device:TPU:1, one launch (start us, length us, event | category | flops | bytes accessed | tf_op | source)
XLA Modules:
  0.0 71.3 jit_solution(9438922408363500275)
XLA Ops:
  0.6 68.8 %sketch_and_gram.1 = (f32[32,256]{1,0:T(8,128)}, f32[256,512]{1,0:T(8,128)}) custom-call(s32[8]{0:T(128)} %order_hbm.1, bf16[512,8,128]{2,1,0:T(8,128)(2,1)} %bitcast.3, s32[2,8,128]{2,1,0:T(8,128)} %flip_hbm.1, s32[32,128]{1,0:T(8,128)} %bitcast.4, s32[32,128]{1,0:T(8,128)} %bitcast.5), custom_call_target="tpu_custom_call" | custom-call | tf_op jit(solution)/shard_map/sketch_and_gram/pallas_call | solution.py:417
  69.5 1.9 %write_out.1 = (f32[32,256]{1,0:T(8,128)}, f32[256,512]{1,0:T(8,128)}) custom-call(f32[32,256]{1,0:T(8,128)} %get-tuple-element.4.sk, f32[256,512]{1,0:T(8,128)} %get-tuple-element.5.gram), custom_call_target="tpu_custom_call" | custom-call | tf_op jit(solution)/shard_map/write_out/pallas_call | solution.py:477

commit v8 on v7

--- a/solution.py
+++ b/solution.py
@@ -47,7 +47,7 @@
 def kernel(
     order_hbm, vol_hbm, flip_hbm, block_hbm, offset_hbm, sk_ref, gram_ref,
     order_ref, flip_ref, block_ref, offset_ref, vol, halo, ext, tables, mover, zs, xs, tt_hi, tt_lo,
-    c, ra1, ra2, rb1, rb2, rz, rv, rw, packed, other, gs, r1, r2, p3, out,
+    c, ra1, ra2, rb1, rb2, rd, rz, rv, rw, packed, other, gs, r1, r2, p3, out,
     ld_sem, sends, a_recv, v_recv, g_recv, recvs,
 ):
     vx, vy, sj = lax.axis_index("vx"), lax.axis_index("vy"), lax.axis_index("subj")
@@ -267,12 +267,19 @@
         for h in range(2):
             at = (*block(h, U, 0, pl.ds(0, 4)), X, lanes_of[h])
             c[at] = c[at] + ra2[u, h, 0] + ra2[u, h, 1]
+            if u == PAIRS - 1:
+                for pos in (2, 1, 3):
+                    src = c.at[(*block(h, U, 0, pos), X, lanes_of[h])]
+                    go(src, rd.at[h, pos - 1], 13, a_recv.at[3, u], second(h, pos))
+                continue
             for k in range(2):
                 part, room = far(u, k)
                 src = c.at[(*block(h, U, 0, 2), part, lanes_of[h])]
                 go(src, rb1.at[u, h, k, :, room], 3, a_recv.at[2, u], second(h, WAYS[k][0]))
 
     def do_b2(u):
+        if u == PAIRS - 1:
+            return
         U = pl.ds(2 * u, 2)
         arrive(rb2.at[u, :, 0], a_recv.at[2, u])
         for h in range(2):
@@ -286,10 +293,14 @@
 
     def do_b3(u):
         U = pl.ds(2 * u, 2)
-        arrive(rb2.at[u], a_recv.at[3, u])
+        last = u == PAIRS - 1
+        arrive(rd if last else rb2.at[u], a_recv.at[3, u])
         for h in range(2):
             at = (U, 0, 0, X, lanes_of[h])
-            c[at] = c[at] + rb2[u, h, 0] + rb2[u, h, 1]
+            if last:
+                c[at] = c[at] + rd[h, 0] + rd[h, 1] + rd[h, 2]
+            else:
+                c[at] = c[at] + rb2[u, h, 0] + rb2[u, h, 1]
         for t in (2 * u, 2 * u + 1):
             o = ORDER[t]
             if o:
@@ -406,8 +417,9 @@
         for i in range(ROWS // 8):
             for j in range(4):
                 gram_ref[q * ROWS + 8 * i : q * ROWS + 8 * i + 8, 128 * j : 128 * j + 128] = out[q, 4 * i + j]
-    whole = (halo, ra1, ra2, rb2.at[:, :, 0], rb2, rz, rv.at[0, :, :, 0], rv.at[pl.ds(1, 3)], rw, other, r1)
-    for kind, ref in enumerate((*whole, r2.at[:, pl.ds(0, RZ - 1)], r1)):
+    ring_b = pl.ds(0, PAIRS - 1)
+    whole = (halo, ra1, ra2, rb2.at[ring_b, :, 0], rb2.at[ring_b], rz, rv.at[0, :, :, 0], rv.at[pl.ds(1, 3)], rw, other, r1)
+    for kind, ref in enumerate((*whole, r2.at[:, pl.ds(0, RZ - 1)], r1, rd)):
         sent(ref, kind)
 
 
@@ -441,6 +453,7 @@
             V((PAIRS, 2, 2, 2, 4, XR, HALF), F32),
             V((PAIRS, 2, 2, 2, 16, HALF), F32),
             V((PAIRS, 2, 2, 2, XR, HALF), F32),
+            V((2, 3, 2, XR, HALF), F32),
             V((RZ - 1, XR, COLS), F32),
             V((4, 2, 2, 2, RX, ZR, COLS), F32),
             V((PLANE - 1, ZR, COLS), F32),
@@ -452,7 +465,7 @@
             V((PARTS, TILES, 8, 128), F32),
             V((PARTS, PLANE * TILES, 8, 128), F32),
             dma((CHUNKS + 4,)),
-            dma((13,)),
+            dma((14,)),
             dma((4, PAIRS)),
             dma((4, 2, 2)),
             dma((3, PARTS)),

time: 71.5 us -> 70.3 us (0.983)
  Pallas kernels: 70.7 us -> 69.5 us
    pallas_call x1, Pallas kernels: 68.8 us -> 67.6 us  [sketch_and_gram(): pl.pallas_call(kernel, out_shape=(jax.ShapeDtypeStruct((KD, COLS), F32),...]
where the time goes in v8:
time: 70.3 us; the launch traced here: 70.1 us
  Pallas kernels  69.5 us (99%)
    pallas_call x1, Pallas kernels, sketch_and_gram(): pl.pallas_call(kernel, out_shape=(jax.ShapeDtypeStruct((KD, COLS), F32),...  67.6 us
    pallas_call x1, Pallas kernels, write_out(): pl.pallas_call(write_kernel, out_shape=(jax.ShapeDtypeStruct(sk.shape, sk...  1.87 us

profile of v8, /device:TPU:1, one launch (start us, length us, event | category | flops | bytes accessed | tf_op | source)
XLA Modules:
  0.0 70.1 jit_solution(16045968678206946259)
XLA Ops:
  0.6 67.6 %sketch_and_gram.1 = (f32[32,256]{1,0:T(8,128)}, f32[256,512]{1,0:T(8,128)}) custom-call(s32[8]{0:T(128)} %order_hbm.1, bf16[512,8,128]{2,1,0:T(8,128)(2,1)} %bitcast.3, s32[2,8,128]{2,1,0:T(8,128)} %flip_hbm.1, s32[32,128]{1,0:T(8,128)} %bitcast.4, s32[32,128]{1,0:T(8,128)} %bitcast.5), custom_call_target="tpu_custom_call" | custom-call | tf_op jit(solution)/shard_map/sketch_and_gram/pallas_call | solution.py:429
  68.3 1.9 %write_out.1 = (f32[32,256]{1,0:T(8,128)}, f32[256,512]{1,0:T(8,128)}) custom-call(f32[32,256]{1,0:T(8,128)} %get-tuple-element.4.sk, f32[256,512]{1,0:T(8,128)} %get-tuple-element.5.gram), custom_call_target="tpu_custom_call" | custom-call | tf_op jit(solution)/shard_map/write_out/pallas_call | solution.py:490

commit v9 on v8

--- a/solution.py
+++ b/solution.py
@@ -189,11 +189,6 @@
             at = slice(k * 128, (k + 1) * 128)
             tables[g, :, at] = jnp.where(pick, wide[:, at], 0.0).astype(BF16)
 
-    lanes = lax.broadcasted_iota(I32, (64, 512), 1)
-    rows = lax.broadcasted_iota(I32, (64, 512), 0)
-    for s in range(8):
-        mover[64 * s : 64 * s + 64, :] = jnp.where(lanes == order_ref[s] * 64 + rows, 1.0, 0.0).astype(BF16)
-
     okx = {-1: jnp.where(vx > 0, 1, 0), 0: 1, 1: jnp.where(vx < PLANE - 1, 1, 0)}
     oky = {-1: jnp.where(vy > 0, 1, 0), 0: 1, 1: jnp.where(vy < RZ - 1, 1, 0)}
     arrive(halo, recvs.at[0])
@@ -339,6 +334,12 @@
             dy, dx = o // RX, o % RX
             go(c.at[t, dy, dx, ZF], rw.at[o - 1], 8, recvs.at[2], xy(dx, dy))
 
+    def column_move():
+        lanes = lax.broadcasted_iota(I32, (64, 512), 1)
+        rows = lax.broadcasted_iota(I32, (64, 512), 0)
+        for s in range(8):
+            mover[64 * s : 64 * s + 64, :] = jnp.where(lanes == order_ref[s] * 64 + rows, 1.0, 0.0).astype(BF16)
+
     stages = ((LAG_A2, do_a2), (LAG_B1, do_b1), (LAG_B2, do_b2), (LAG_B3, do_b3))
     ring_at = {1: 0, 2: 2, 3: 4, 4: 6}
     for step in range(PAIRS + LAG_B3):
@@ -348,6 +349,8 @@
                 ring(1)
             contribute(2 * step + 1)
             start_a1(step)
+        elif step == PAIRS:
+            column_move()
         for n in (2, 3, 4):
             if ring_at[n] == step:
                 ring(n)

time: 70.3 us -> 70.1 us (level)
  no operation moved by 1% of the time
where the time goes in v9:
time: 70.1 us; the launch traced here: 70 us
  Pallas kernels  69.3 us (99%)
    pallas_call x1, Pallas kernels, sketch_and_gram(): pl.pallas_call(kernel, out_shape=(jax.ShapeDtypeStruct((KD, COLS), F32),...  67.5 us
    pallas_call x1, Pallas kernels, write_out(): pl.pallas_call(write_kernel, out_shape=(jax.ShapeDtypeStruct(sk.shape, sk...  1.87 us

profile of v9, /device:TPU:1, one launch (start us, length us, event | category | flops | bytes accessed | tf_op | source)
XLA Modules:
  0.0 70.0 jit_solution(14811224024552683411)
XLA Ops:
  0.6 67.5 %sketch_and_gram.1 = (f32[32,256]{1,0:T(8,128)}, f32[256,512]{1,0:T(8,128)}) custom-call(s32[8]{0:T(128)} %order_hbm.1, bf16[512,8,128]{2,1,0:T(8,128)(2,1)} %bitcast.3, s32[2,8,128]{2,1,0:T(8,128)} %flip_hbm.1, s32[32,128]{1,0:T(8,128)} %bitcast.4, s32[32,128]{1,0:T(8,128)} %bitcast.5), custom_call_target="tpu_custom_call" | custom-call | tf_op jit(solution)/shard_map/sketch_and_gram/pallas_call | solution.py:432
  68.1 1.9 %write_out.1 = (f32[32,256]{1,0:T(8,128)}, f32[256,512]{1,0:T(8,128)}) custom-call(f32[32,256]{1,0:T(8,128)} %get-tuple-element.4.sk, f32[256,512]{1,0:T(8,128)} %get-tuple-element.5.gram), custom_call_target="tpu_custom_call" | custom-call | tf_op jit(solution)/shard_map/write_out/pallas_call | solution.py:493
